TPU v7x, 128 devices: a whole 4x4x4 slice. The times are simulated.
128 devices in a mesh: expert: 8 (over x, core), tensor: 16 (over y, z).
Axes of the slice: x: 4, y: 4, z: 4, core: 2. Of those that a mesh axis runs over, the one named last changes fastest.
Arguments:
- tokens: bfloat16 [16384, 2048], P(('expert', 'tensor')), may hold values from -6 to 6
- expert_ids: int32 [16384, 8], P(('expert', 'tensor')), may hold values from 0 to 127, all different within a row; in each aligned block of 128 rows (0 to 127, 128 to 255, ...) at most 16 rows name the same one
- route_gates: float32 [16384, 8], P(('expert', 'tensor')), may hold values from 0.05 to 0.45
- expert_weights: bfloat16 [128, 3, 768, 2048], P('expert', None, 'tensor'), may hold values from -0.125 to 0.125
Outputs:
- combined: bfloat16 [16384, 2048], P(('expert', 'tensor'))
Inputs may be any that keep to these rules, and one draw needn't show every extreme that they name: `expert_ids`: each row names 8 different experts; within the 128 rows of one device (aligned blocks) no expert is named by more than 16 rows, a bound that some block reaches.
All inputs are finite; a program needn't handle non-finite values.
Results may differ from a plain program's by a relative error of at most 0.015.
Values may be sent and summed in bfloat16 or wider, within the bound.
No kernel may reach another device: no remote copies, remote signals or barrier semaphores. Data moves between devices by JAX's collectives and lax.ppermute only.
A program may use at most 192 MiB of HBM per device.

v0:
```python
import jax
import jax.numpy as jnp
from jax import lax
from jax.sharding import PartitionSpec as P

MOST = 16


def expert_block(full_weights, owned_rows, block_count):
    gate_up = jnp.einsum(
        "ekhd,erd->ekhr", full_weights[:, 0:2], owned_rows, preferred_element_type=jnp.float32
    )
    hidden = (jax.nn.silu(gate_up[:, 0]) * gate_up[:, 1]).astype(jnp.bfloat16)
    owned = full_weights.shape[0]
    full_width = full_weights.shape[2]
    block_width = full_width // block_count
    row_count = owned_rows.shape[1]
    model_width = owned_rows.shape[2]
    hidden_blocks = jnp.moveaxis(hidden.reshape(owned, block_count, block_width, row_count), 1, 0)
    down_blocks = jnp.moveaxis(
        full_weights[:, 2].reshape(owned, block_count, block_width, model_width), 1, 0
    )

    def add_block(total, operand):
        hidden_part, down_part = operand
        term = jnp.einsum(
            "ehr,ehd->erd", hidden_part, down_part, preferred_element_type=jnp.float32
        )
        return (total + term.astype(jnp.bfloat16).astype(jnp.float32), None)

    start_total = jnp.zeros((owned, row_count, model_width), jnp.float32)
    total, unused = lax.scan(add_block, start_total, (hidden_blocks, down_blocks))
    return total.astype(jnp.bfloat16)


def body(tokens, expert_ids, route_gates, expert_weights):
    tok_rows, top_count = expert_ids.shape
    groups = lax.axis_size("expert")
    tensor_count = lax.axis_size("tensor")
    local_experts = expert_weights.shape[0]
    experts_all = local_experts * groups
    model_width = tokens.shape[1]
    flat_ids = expert_ids.reshape(-1)
    onehot = (flat_ids[:, None] == jnp.arange(experts_all, dtype=jnp.int32)[None, :]).astype(
        jnp.int32
    )
    ranked = jnp.sum((jnp.cumsum(onehot, axis=0) - onehot) * onehot, axis=1)
    slot_index = flat_ids * MOST + ranked
    slot_grid = slot_index.reshape(tok_rows, top_count)
    dispatch_table = jnp.any(
        slot_grid[None, :, :] == jnp.arange(experts_all * MOST, dtype=jnp.int32)[:, None, None],
        axis=2,
    ).astype(jnp.bfloat16)
    outgoing = jnp.dot(dispatch_table, tokens, preferred_element_type=jnp.float32).astype(
        jnp.bfloat16
    )
    outgoing = outgoing.reshape(experts_all, MOST, model_width)
    full_weights = lax.all_to_all(expert_weights, "tensor", split_axis=0, concat_axis=2, tiled=True)
    arrived = lax.all_to_all(outgoing, "expert", split_axis=0, concat_axis=1, tiled=True)
    owned_rows = lax.all_to_all(arrived, "tensor", split_axis=0, concat_axis=1, tiled=True)
    outputs = expert_block(full_weights, owned_rows, tensor_count)
    results = lax.all_to_all(outputs, "tensor", split_axis=1, concat_axis=0, tiled=True)
    returned = lax.all_to_all(results, "expert", split_axis=1, concat_axis=0, tiled=True)
    picked = returned.reshape(experts_all * MOST, model_width)[slot_index]
    picked = picked.astype(jnp.float32).reshape(tok_rows, top_count, model_width)
    combined = jnp.sum(route_gates[:, :, None] * picked, axis=1)
    return combined.astype(jnp.bfloat16)


def solution(mesh):
    in_specs = (
        P(("expert", "tensor"), None),
        P(("expert", "tensor"), None),
        P(("expert", "tensor"), None),
        P("expert", None, "tensor", None),
    )
    out_specs = P(("expert", "tensor"), None)
    return jax.shard_map(body, mesh=mesh, in_specs=in_specs, out_specs=out_specs, check_vma=False)
```

profile of v0, /device:TPU:6, one launch (start us, length us, event | category | flops | bytes accessed | tf_op | source)
XLA Modules:
  0.0 1080.4 jit_solution(924796779361198566)
XLA Ops:
  13.1 98.5 %all_to_all.72 = bf16[128,16,2048]{2,1,0:T(8,128)(2,1)} all-to-all(bf16[128,16,2048]{2,1,0:T(8,128)(2,1)S(1)} %bitcast.76), channel_id=1, replica_groups=mesh['expert'=8,'tensor'=16] {'expert'}, dimensions={0} | all-to-all | bytes 16777216 | tf_op jit(solution)/shard_map/all_to_all | solution.py:59
  128.0 155.8 %all-to-all-done.2 = bf16[16,3,48,2048]{3,2,1,0:T(8,128)(2,1)} async-done(((bf16[16,3,48,2048]{3,2,1,0:T(8,128)(2,1)}), bf16[16,3,48,2048]{3,2,1,0:T(8,128)(2,1)}, u32[]{:S(2)}, u32[]{:S(2)}) %all-to-all-start.2) | async-done | bytes 9437216 | tf_op jit(solution)/shard_map/all_to_all | solution.py:58
  307.0 106.6 %all-to-all-done.1 = bf16[16,128,2048]{2,1,0:T(8,128)(2,1)} async-done(((bf16[16,128,2048]{2,1,0:T(8,128)(2,1)}), bf16[16,128,2048]{2,1,0:T(8,128)(2,1)}, u32[]{:S(2)}, u32[]{:S(2)}) %all-to-all-start.1) | async-done | bytes 8388640 | tf_op jit(solution)/shard_map/all_to_all | solution.py:60
  413.6 19.2 %fusion.8 = f32[1,2,768,2048]{3,2,1,0:T(8,128)} fusion(bf16[2048,2048,1]{1,0,2:T(8,128)(2,1)} %bitcast.8, bf16[1,3,768,2048]{3,2,1,0:T(8,128)(2,1)} %bitcast.83), kind=kOutput, calls=%fused_computation.15 | convolution fusion | flops 12884901888 | bytes 27262976 | tf_op jit(solution)/shard_map/ekhd,erd->ekhr/dot_general | solution.py:10
  432.7 11.4 %fusion.15 = (f32[1,1,768,2048]{3,2,1,0:T(8,128)}, f32[1,1,768,2048]{3,2,1,0:T(8,128)}) fusion(f32[1,2,768,2048]{3,2,1,0:T(8,128)} %fusion.8), kind=kLoop, calls=%fused_computation.30 | loop fusion | bytes 25165824 | tf_op jit(solution)/shard_map/slice | solution.py:13
  450.9 220.3 %while.11 = (s32[]{:T(128)}, f32[1,2048,2048]{2,1,0:T(8,128)}, bf16[16,1,48,2048]{3,2,1,0:T(8,128)(2,1)}, bf16[16,1,48,2048]{3,2,1,0:T(8,128)(2,1)}, s32[]{:T(128)}, /*index=5*/s32[]{:T(128)}) while((s32[]{:T(128)}, f32[1,2048,2048]{2,1,0:T(8,128)}, bf16[16,1,48,2048]{3,2,1,0:T(8,128)(2,1)}, bf16[16,1,48,2048]{3,2,1,0:T(8,128)(2,1)}, ...), condition=%wide.region_5.6_spmd.clone, body=%wide.region_4.5_spmd.clone.sunk | while | flops 419430400 | bytes 33948748 | solution.py:32
  460.0 14.1 %convert_add_fusion.2 = f32[1,2048,2048]{2,1,0:T(8,128)} fusion(f32[1,2048,2048]{2,1,0:T(8,128)} %get-tuple-element.107, pred[]{:T(512)S(6)} %compare.3, bf16[16,1,48,2048]{3,2,1,0:T(8,128)(2,1)} %get-tuple-element.115, s32[]{:T(128)} %get-tuple-element.106, bf16[16,1,48,2048]{3,2,1,0:T(8,128)(2,1)} %get-tuple-element.114), kind=kOutput, calls=%fused_computation.1.clone.1 | convolution fusion | flops 419430400 | bytes 33948672 | tf_op jit(solution)/shard_map/while/body/eval_jaxpr/ehr,ehd->erd/dot_general | solution.py:26
  474.1 14.1 %convert_add_fusion.2 = f32[1,2048,2048]{2,1,0:T(8,128)} fusion(f32[1,2048,2048]{2,1,0:T(8,128)} %get-tuple-element.107, pred[]{:T(512)S(6)} %compare.3, bf16[16,1,48,2048]{3,2,1,0:T(8,128)(2,1)} %get-tuple-element.115, s32[]{:T(128)} %get-tuple-element.106, bf16[16,1,48,2048]{3,2,1,0:T(8,128)(2,1)} %get-tuple-element.114), kind=kOutput, calls=%fused_computation.1.clone.1 | convolution fusion | flops 419430400 | bytes 33948672 | tf_op jit(solution)/shard_map/while/body/eval_jaxpr/ehr,ehd->erd/dot_general | solution.py:26
  488.2 14.1 %convert_add_fusion.2 = f32[1,2048,2048]{2,1,0:T(8,128)} fusion(f32[1,2048,2048]{2,1,0:T(8,128)} %get-tuple-element.107, pred[]{:T(512)S(6)} %compare.3, bf16[16,1,48,2048]{3,2,1,0:T(8,128)(2,1)} %get-tuple-element.115, s32[]{:T(128)} %get-tuple-element.106, bf16[16,1,48,2048]{3,2,1,0:T(8,128)(2,1)} %get-tuple-element.114), kind=kOutput, calls=%fused_computation.1.clone.1 | convolution fusion | flops 419430400 | bytes 33948672 | tf_op jit(solution)/shard_map/while/body/eval_jaxpr/ehr,ehd->erd/dot_general | solution.py:26
  502.3 14.1 %convert_add_fusion.2 = f32[1,2048,2048]{2,1,0:T(8,128)} fusion(f32[1,2048,2048]{2,1,0:T(8,128)} %get-tuple-element.107, pred[]{:T(512)S(6)} %compare.3, bf16[16,1,48,2048]{3,2,1,0:T(8,128)(2,1)} %get-tuple-element.115, s32[]{:T(128)} %get-tuple-element.106, bf16[16,1,48,2048]{3,2,1,0:T(8,128)(2,1)} %get-tuple-element.114), kind=kOutput, calls=%fused_computation.1.clone.1 | convolution fusion | flops 419430400 | bytes 33948672 | tf_op jit(solution)/shard_map/while/body/eval_jaxpr/ehr,ehd->erd/dot_general | solution.py:26
  516.3 14.1 %convert_add_fusion.2 = f32[1,2048,2048]{2,1,0:T(8,128)} fusion(f32[1,2048,2048]{2,1,0:T(8,128)} %get-tuple-element.107, pred[]{:T(512)S(6)} %compare.3, bf16[16,1,48,2048]{3,2,1,0:T(8,128)(2,1)} %get-tuple-element.115, s32[]{:T(128)} %get-tuple-element.106, bf16[16,1,48,2048]{3,2,1,0:T(8,128)(2,1)} %get-tuple-element.114), kind=kOutput, calls=%fused_computation.1.clone.1 | convolution fusion | flops 419430400 | bytes 33948672 | tf_op jit(solution)/shard_map/while/body/eval_jaxpr/ehr,ehd->erd/dot_general | solution.py:26
  530.4 14.1 %convert_add_fusion.2 = f32[1,2048,2048]{2,1,0:T(8,128)} fusion(f32[1,2048,2048]{2,1,0:T(8,128)} %get-tuple-element.107, pred[]{:T(512)S(6)} %compare.3, bf16[16,1,48,2048]{3,2,1,0:T(8,128)(2,1)} %get-tuple-element.115, s32[]{:T(128)} %get-tuple-element.106, bf16[16,1,48,2048]{3,2,1,0:T(8,128)(2,1)} %get-tuple-element.114), kind=kOutput, calls=%fused_computation.1.clone.1 | convolution fusion | flops 419430400 | bytes 33948672 | tf_op jit(solution)/shard_map/while/body/eval_jaxpr/ehr,ehd->erd/dot_general | solution.py:26
  544.5 14.1 %convert_add_fusion.2 = f32[1,2048,2048]{2,1,0:T(8,128)} fusion(f32[1,2048,2048]{2,1,0:T(8,128)} %get-tuple-element.107, pred[]{:T(512)S(6)} %compare.3, bf16[16,1,48,2048]{3,2,1,0:T(8,128)(2,1)} %get-tuple-element.115, s32[]{:T(128)} %get-tuple-element.106, bf16[16,1,48,2048]{3,2,1,0:T(8,128)(2,1)} %get-tuple-element.114), kind=kOutput, calls=%fused_computation.1.clone.1 | convolution fusion | flops 419430400 | bytes 33948672 | tf_op jit(solution)/shard_map/while/body/eval_jaxpr/ehr,ehd->erd/dot_general | solution.py:26
  558.6 14.1 %convert_add_fusion.2 = f32[1,2048,2048]{2,1,0:T(8,128)} fusion(f32[1,2048,2048]{2,1,0:T(8,128)} %get-tuple-element.107, pred[]{:T(512)S(6)} %compare.3, bf16[16,1,48,2048]{3,2,1,0:T(8,128)(2,1)} %get-tuple-element.115, s32[]{:T(128)} %get-tuple-element.106, bf16[16,1,48,2048]{3,2,1,0:T(8,128)(2,1)} %get-tuple-element.114), kind=kOutput, calls=%fused_computation.1.clone.1 | convolution fusion | flops 419430400 | bytes 33948672 | tf_op jit(solution)/shard_map/while/body/eval_jaxpr/ehr,ehd->erd/dot_general | solution.py:26
  572.7 14.1 %convert_add_fusion.2 = f32[1,2048,2048]{2,1,0:T(8,128)} fusion(f32[1,2048,2048]{2,1,0:T(8,128)} %get-tuple-element.107, pred[]{:T(512)S(6)} %compare.3, bf16[16,1,48,2048]{3,2,1,0:T(8,128)(2,1)} %get-tuple-element.115, s32[]{:T(128)} %get-tuple-element.106, bf16[16,1,48,2048]{3,2,1,0:T(8,128)(2,1)} %get-tuple-element.114), kind=kOutput, calls=%fused_computation.1.clone.1 | convolution fusion | flops 419430400 | bytes 33948672 | tf_op jit(solution)/shard_map/while/body/eval_jaxpr/ehr,ehd->erd/dot_general | solution.py:26
  586.7 14.1 %convert_add_fusion.2 = f32[1,2048,2048]{2,1,0:T(8,128)} fusion(f32[1,2048,2048]{2,1,0:T(8,128)} %get-tuple-element.107, pred[]{:T(512)S(6)} %compare.3, bf16[16,1,48,2048]{3,2,1,0:T(8,128)(2,1)} %get-tuple-element.115, s32[]{:T(128)} %get-tuple-element.106, bf16[16,1,48,2048]{3,2,1,0:T(8,128)(2,1)} %get-tuple-element.114), kind=kOutput, calls=%fused_computation.1.clone.1 | convolution fusion | flops 419430400 | bytes 33948672 | tf_op jit(solution)/shard_map/while/body/eval_jaxpr/ehr,ehd->erd/dot_general | solution.py:26
  600.8 14.1 %convert_add_fusion.2 = f32[1,2048,2048]{2,1,0:T(8,128)} fusion(f32[1,2048,2048]{2,1,0:T(8,128)} %get-tuple-element.107, pred[]{:T(512)S(6)} %compare.3, bf16[16,1,48,2048]{3,2,1,0:T(8,128)(2,1)} %get-tuple-element.115, s32[]{:T(128)} %get-tuple-element.106, bf16[16,1,48,2048]{3,2,1,0:T(8,128)(2,1)} %get-tuple-element.114), kind=kOutput, calls=%fused_computation.1.clone.1 | convolution fusion | flops 419430400 | bytes 33948672 | tf_op jit(solution)/shard_map/while/body/eval_jaxpr/ehr,ehd->erd/dot_general | solution.py:26
  614.9 14.1 %convert_add_fusion.2 = f32[1,2048,2048]{2,1,0:T(8,128)} fusion(f32[1,2048,2048]{2,1,0:T(8,128)} %get-tuple-element.107, pred[]{:T(512)S(6)} %compare.3, bf16[16,1,48,2048]{3,2,1,0:T(8,128)(2,1)} %get-tuple-element.115, s32[]{:T(128)} %get-tuple-element.106, bf16[16,1,48,2048]{3,2,1,0:T(8,128)(2,1)} %get-tuple-element.114), kind=kOutput, calls=%fused_computation.1.clone.1 | convolution fusion | flops 419430400 | bytes 33948672 | tf_op jit(solution)/shard_map/while/body/eval_jaxpr/ehr,ehd->erd/dot_general | solution.py:26
  629.0 14.1 %convert_add_fusion.2 = f32[1,2048,2048]{2,1,0:T(8,128)} fusion(f32[1,2048,2048]{2,1,0:T(8,128)} %get-tuple-element.107, pred[]{:T(512)S(6)} %compare.3, bf16[16,1,48,2048]{3,2,1,0:T(8,128)(2,1)} %get-tuple-element.115, s32[]{:T(128)} %get-tuple-element.106, bf16[16,1,48,2048]{3,2,1,0:T(8,128)(2,1)} %get-tuple-element.114), kind=kOutput, calls=%fused_computation.1.clone.1 | convolution fusion | flops 419430400 | bytes 33948672 | tf_op jit(solution)/shard_map/while/body/eval_jaxpr/ehr,ehd->erd/dot_general | solution.py:26
  643.1 14.1 %convert_add_fusion.2 = f32[1,2048,2048]{2,1,0:T(8,128)} fusion(f32[1,2048,2048]{2,1,0:T(8,128)} %get-tuple-element.107, pred[]{:T(512)S(6)} %compare.3, bf16[16,1,48,2048]{3,2,1,0:T(8,128)(2,1)} %get-tuple-element.115, s32[]{:T(128)} %get-tuple-element.106, bf16[16,1,48,2048]{3,2,1,0:T(8,128)(2,1)} %get-tuple-element.114), kind=kOutput, calls=%fused_computation.1.clone.1 | convolution fusion | flops 419430400 | bytes 33948672 | tf_op jit(solution)/shard_map/while/body/eval_jaxpr/ehr,ehd->erd/dot_general | solution.py:26
  657.1 14.1 %convert_add_fusion.2 = f32[1,2048,2048]{2,1,0:T(8,128)} fusion(f32[1,2048,2048]{2,1,0:T(8,128)} %get-tuple-element.107, pred[]{:T(512)S(6)} %compare.3, bf16[16,1,48,2048]{3,2,1,0:T(8,128)(2,1)} %get-tuple-element.115, s32[]{:T(128)} %get-tuple-element.106, bf16[16,1,48,2048]{3,2,1,0:T(8,128)(2,1)} %get-tuple-element.114), kind=kOutput, calls=%fused_computation.1.clone.1 | convolution fusion | flops 419430400 | bytes 33948672 | tf_op jit(solution)/shard_map/while/body/eval_jaxpr/ehr,ehd->erd/dot_general | solution.py:26
  677.8 48.4 %copy.78 = bf16[1,2048,2048]{2,0,1:T(2,128)(2,1)} copy(bf16[1,2048,2048]{2,1,0:T(8,128)(2,1)S(1)} %convert_element_type.50) | data formatting | bytes 16777216 | tf_op jit(solution)/shard_map/convert_element_type | solution.py:33
  726.6 51.1 %reduce = bf16[2048,2048]{1,0:T(8,128)(2,1)} reduce(bf16[2048,1,2048]{2,1,0:T(2,128)(2,1)} %bitcast.75, bf16[]{:T(256)} %broadcast.75), dimensions={1}, to_apply=%bitcast.66.reduce_sub_computation | reduce | bytes 16777218
  777.7 14.5 %reshape.164 = bf16[16,2,131072]{2,1,0:T(2,128)(2,1)} reshape(bf16[2048,2048]{1,0:T(8,128)(2,1)} %reduce) | data formatting | bytes 16777216
  792.3 98.3 %all_to_all.73 = bf16[16,2,131072]{2,1,0:T(2,128)(2,1)} all-to-all(bf16[16,2,131072]{2,1,0:T(2,128)(2,1)} %reshape.164), channel_id=1, replica_groups=mesh['expert'=8,'tensor'=16] {'tensor'}, dimensions={0} | all-to-all | bytes 16777216 | tf_op jit(solution)/shard_map/all_to_all | solution.py:62
  890.6 16.3 %reshape.165 = bf16[2048,1,2048]{2,1,0:T(2,128)(2,1)} reshape(bf16[16,2,131072]{2,1,0:T(2,128)(2,1)} %all_to_all.73) | data formatting | bytes 16777216
  907.0 13.5 %copy.76 = bf16[1,2048,2048]{2,1,0:T(8,128)(2,1)} copy(bf16[1,2048,2048]{2,0,1:T(2,128)(2,1)} %bitcast.74) | data formatting | bytes 16777216
  920.4 11.2 %copy.72 = bf16[16,128,2048]{2,0,1:T(8,128)(2,1)} copy(bf16[16,128,2048]{2,1,0:T(8,128)(2,1)} %bitcast.77) | data formatting | bytes 16777216 | tf_op jit(solution)/shard_map/all_to_all | solution.py:62
  931.7 23.2 %all-to-all-start.4 = ((bf16[16,128,2048]{2,0,1:T(8,128)(2,1)}), bf16[16,128,2048]{2,0,1:T(8,128)(2,1)}, u32[]{:S(2)}, u32[]{:S(2)}) async-start(bf16[16,128,2048]{2,0,1:T(8,128)(2,1)} %copy.72), calls=%async_computation.4 | async-start | bytes 16777216 | tf_op jit(solution)/shard_map/all_to_all | solution.py:63
  955.1 92.3 %all-to-all-done.4 = bf16[16,128,2048]{2,0,1:T(8,128)(2,1)} async-done(((bf16[16,128,2048]{2,0,1:T(8,128)(2,1)}), bf16[16,128,2048]{2,0,1:T(8,128)(2,1)}, u32[]{:S(2)}, u32[]{:S(2)}) %all-to-all-start.4) | async-done | bytes 8388640 | tf_op jit(solution)/shard_map/all_to_all | solution.py:63
  1047.4 12.1 %copy.74 = bf16[8,16,16,2048]{3,2,1,0:T(8,128)(2,1)} copy(bf16[8,16,16,2048]{3,1,2,0:T(8,128)(2,1)} %bitcast.25) | data formatting | bytes 16777216 | tf_op jit(solution)/shard_map/all_to_all | solution.py:63
  1059.5 13.3 %gather_fusion = bf16[1024,2048]{1,0:T(8,128)(2,1)} fusion(bf16[2048,2048]{1,0:T(8,128)(2,1)} %bitcast.73, s32[1024]{0:T(1024)S(1)} %broadcast_clamp_fusion), kind=kCustom, calls=%fused_computation | custom fusion | bytes 8392704 | tf_op jit(solution)/shard_map/gather | solution.py:64
  (43 shorter events, 83.0 us)
Async XLA Ops:
  0.0 10.7 copy-start
  1.9 0.6 copy-start.3
  111.6 172.2 %all-to-all-start.2 = ((bf16[16,3,48,2048]{3,2,1,0:T(8,128)(2,1)}), bf16[16,3,48,2048]{3,2,1,0:T(8,128)(2,1)}, u32[]{:S(2)}, u32[]{:S(2)}) async-start(bf16[16,3,48,2048]{3,2,1,0:T(8,128)(2,1)} %param.9), calls=%async_computation.2 | async-start | bytes 18874368 | tf_op jit(solution)/shard_map/all_to_all | solution.py:58
  283.8 129.7 %all-to-all-start.1 = ((bf16[16,128,2048]{2,1,0:T(8,128)(2,1)}), bf16[16,128,2048]{2,1,0:T(8,128)(2,1)}, u32[]{:S(2)}, u32[]{:S(2)}) async-start(bf16[16,128,2048]{2,1,0:T(8,128)(2,1)} %bitcast.78), calls=%async_computation.1 | async-start | bytes 16777216 | tf_op jit(solution)/shard_map/all_to_all | solution.py:60
  931.7 23.2 %copy-start.2 = (s32[128,8]{1,0:T(8,128)S(1)}, s32[128,8]{1,0:T(8,128)}, u32[]{:S(2)}) copy-start(s32[128,8]{1,0:T(8,128)} %get-tuple-element.73) | copy-start | bytes 12292
  931.7 23.3 %copy-start.5 = (f32[128,8]{0,1:T(8,128)S(1)}, f32[128,8]{0,1:T(8,128)}, u32[]{:S(2)}) copy-start(f32[128,8]{0,1:T(8,128)} %param.8) | copy-start | bytes 12292
  931.7 23.4 %copy-start.4 = (s32[1024]{0:T(1024)S(1)}, s32[1024]{0:T(1024)}, u32[]{:S(2)}) copy-start(s32[1024]{0:T(1024)} %copy-done.3) | copy-start | bytes 12292
  931.7 115.7 %all-to-all-start.4 = ((bf16[16,128,2048]{2,0,1:T(8,128)(2,1)}), bf16[16,128,2048]{2,0,1:T(8,128)(2,1)}, u32[]{:S(2)}, u32[]{:S(2)}) async-start(bf16[16,128,2048]{2,0,1:T(8,128)(2,1)} %copy.72), calls=%async_computation.4 | async-start | bytes 16777216 | tf_op jit(solution)/shard_map/all_to_all | solution.py:63
  1059.5 20.7 %copy-start.1 = (bf16[128,2048]{1,0:T(8,128)(2,1)S(1)}, bf16[128,2048]{1,0:T(8,128)(2,1)}, u32[]{:S(2)}) copy-start(bf16[128,2048]{1,0:T(8,128)(2,1)} %param.6) | copy-start | bytes 1572868
where the time goes:
time: 1090 us; the launch traced here: 1080 us
  waiting for transfers between devices  355 us (33%)
  matrix products  242 us (22%)
  blocking collectives  197 us (18%)
  local copies, waits for them, and re-layouts  165 us (15%)
  other arithmetic  80.5 us (7%)
  starting transfers between devices  41.2 us (4%)
    dot_general x16, matrix products, add_block(): jnp.einsum('ehr,ehd->erd', hidden_part, down_part, preferred_element_type...  220 us
    all_to_all x1, waiting for transfers between devices, body(): lax.all_to_all(expert_weights, 'tensor', split_axis=0, concat_axis=2, til...  156 us
    all_to_all x1, waiting for transfers between devices, body(): lax.all_to_all(arrived, 'tensor', split_axis=0, concat_axis=1, tiled=True)  107 us
    all_to_all x1, blocking collectives, body(): lax.all_to_all(outgoing, 'expert', split_axis=0, concat_axis=1, tiled=True)  98.5 us
    all_to_all x1, blocking collectives, body(): lax.all_to_all(outputs, 'tensor', split_axis=1, concat_axis=0, tiled=True)  98.3 us
    all_to_all x1, waiting for transfers between devices, body(): lax.all_to_all(results, 'expert', split_axis=1, concat_axis=0, tiled=True)  92.3 us
    unnamed x2, other arithmetic  51.1 us
    convert_element_type x1, local copies, waits for them, and re-layouts, expert_block(): return total.astype(jnp.bfloat16)  48.4 us
  transfers between devices with their start and end apart: 3, of which 3 were waited for; matrix products, arithmetic and copies ran while one was open for 2% of the time, Pallas kernels for 0%

commit v1 on v0

v1 whole, which is shorter than its diff:
```python
import jax
import jax.numpy as jnp
from jax import lax
from jax.experimental import pallas as pl
from jax.experimental.pallas import tpu as pltpu
from jax.sharding import PartitionSpec as P

MOST = 16
AXES = ("expert", "tensor")


def slot_codes(ids_t, experts):
    top, rows = ids_t.shape
    names = lax.broadcasted_iota(jnp.int32, (experts, rows), 0)
    member = names == ids_t[0:1, :]
    for k in range(1, top):
        member = member | (names == ids_t[k : k + 1, :])
    before = lax.broadcasted_iota(jnp.int32, (rows, rows), 0) < lax.broadcasted_iota(
        jnp.int32, (rows, rows), 1
    )
    rank = jnp.dot(
        member.astype(jnp.float32).astype(jnp.bfloat16),
        before.astype(jnp.float32).astype(jnp.bfloat16),
        preferred_element_type=jnp.float32,
    )
    return jnp.where(member, rank, -1.0)


def dispatch_kernel(ids_ref, tokens_ref, out_ref, code_ref):
    part = out_ref.shape[0]
    step = pl.program_id(0)

    @pl.when(step == 0)
    def _():
        code_ref[...] = slot_codes(ids_ref[...], code_ref.shape[0])

    code = code_ref[pl.ds(pl.multiple_of(step * part, part), part), :]
    rows = code.shape[1]
    slots = lax.broadcasted_iota(jnp.int32, (part, MOST, rows), 1).astype(jnp.float32)
    pick = jnp.where(code[:, None, :] == slots, 1.0, 0.0)
    pick = pick.reshape(part * MOST, rows).astype(jnp.bfloat16)
    picked = jnp.dot(pick, tokens_ref[...], preferred_element_type=jnp.float32)
    out_ref[...] = picked.astype(jnp.bfloat16).reshape(out_ref.shape)


def dispatch(ids_t, tokens, experts):
    rows, width = tokens.shape
    part = 16
    return pl.pallas_call(
        dispatch_kernel,
        out_shape=jax.ShapeDtypeStruct((experts, MOST, width), jnp.bfloat16),
        grid=(experts // part,),
        in_specs=[
            pl.BlockSpec(ids_t.shape, lambda i: (0, 0)),
            pl.BlockSpec((rows, width), lambda i: (0, 0)),
        ],
        out_specs=pl.BlockSpec((part, MOST, width), lambda i: (i, 0, 0)),
        scratch_shapes=[pltpu.VMEM((experts, rows), jnp.float32)],
        compiler_params=pltpu.CompilerParams(vmem_limit_bytes=32 << 20),
        cost_estimate=pl.CostEstimate(
            flops=2 * experts * MOST * rows * width,
            bytes_accessed=2 * (experts * MOST + rows) * width,
            transcendentals=0,
        ),
        name="dispatch",
    )(ids_t, tokens)


def ffn_kernel(rows_ref, weights_ref, out_ref):
    blocks, _, width_block, model = weights_ref.shape
    hidden_units = blocks * width_block
    contract_last = (((1,), (1,)), ((), ()))
    x = rows_ref[...]
    w_gate = weights_ref[:, 0].reshape(hidden_units, model)
    w_up = weights_ref[:, 1].reshape(hidden_units, model)
    w_down = weights_ref[:, 2].reshape(hidden_units, model)
    gate = lax.dot_general(x, w_gate, contract_last, preferred_element_type=jnp.float32)
    up = lax.dot_general(x, w_up, contract_last, preferred_element_type=jnp.float32)
    hidden = (gate / (1.0 + jnp.exp(-gate)) * up).astype(jnp.bfloat16)
    out_ref[...] = jnp.dot(hidden, w_down, preferred_element_type=jnp.float32).astype(jnp.bfloat16)


def expert_ffn(rows, weights):
    count, model = rows.shape
    part = 256
    return pl.pallas_call(
        ffn_kernel,
        out_shape=jax.ShapeDtypeStruct((count, model), jnp.bfloat16),
        grid=(count // part,),
        in_specs=[
            pl.BlockSpec((part, model), lambda i: (i, 0)),
            pl.BlockSpec(weights.shape, lambda i: (0, 0, 0, 0), pipeline_mode=pl.Buffered(1)),
        ],
        out_specs=pl.BlockSpec((part, model), lambda i: (i, 0)),
        compiler_params=pltpu.CompilerParams(vmem_limit_bytes=48 << 20),
        cost_estimate=pl.CostEstimate(
            flops=2 * count * weights.size,
            bytes_accessed=2 * (2 * rows.size + weights.size),
            transcendentals=count * weights.size // (3 * model),
        ),
        name="expert_ffn",
    )(rows, weights)


def combine_kernel(ids_ref, gates_ref, rows_ref, out_ref, total_ref, code_ref, gate_ref):
    part = rows_ref.shape[0]
    step = pl.program_id(0)

    @pl.when(step == 0)
    def _():
        ids_t = ids_ref[...]
        experts, rows = code_ref.shape
        code_ref[...] = slot_codes(ids_t, experts)
        names = lax.broadcasted_iota(jnp.int32, (experts, rows), 0)
        gate = jnp.zeros((experts, rows), jnp.float32)
        for k in range(ids_t.shape[0]):
            gate = jnp.where(names == ids_t[k : k + 1, :], gates_ref[k : k + 1, :], gate)
        gate_ref[...] = gate
        total_ref[...] = jnp.zeros_like(total_ref)

    here = pl.ds(pl.multiple_of(step * part, part), part)
    code = code_ref[here, :]
    gate = gate_ref[here, :]
    rows = code.shape[1]
    slots = lax.broadcasted_iota(jnp.int32, (part, MOST, rows), 1).astype(jnp.float32)
    weight = jnp.where(code[:, None, :] == slots, gate[:, None, :], 0.0)
    weight = weight.reshape(part * MOST, rows)
    high = weight.astype(jnp.bfloat16)
    low = (weight - high.astype(jnp.float32)).astype(jnp.bfloat16)
    both = jnp.concatenate([high, low], axis=1)
    values = rows_ref[...].reshape(part * MOST, rows_ref.shape[2])
    sums = lax.dot_general(
        both, values, (((0,), (0,)), ((), ())), preferred_element_type=jnp.float32
    )
    total_ref[...] += sums[:rows] + sums[rows:]

    @pl.when(step == pl.num_programs(0) - 1)
    def _():
        out_ref[...] = total_ref[...].astype(jnp.bfloat16)


def combine(ids_t, gates_t, returned):
    experts, most, width = returned.shape
    rows = ids_t.shape[1]
    part = 16
    return pl.pallas_call(
        combine_kernel,
        out_shape=jax.ShapeDtypeStruct((rows, width), jnp.bfloat16),
        grid=(experts // part,),
        in_specs=[
            pl.BlockSpec(ids_t.shape, lambda i: (0, 0)),
            pl.BlockSpec(gates_t.shape, lambda i: (0, 0)),
            pl.BlockSpec((part, most, width), lambda i: (i, 0, 0)),
        ],
        out_specs=pl.BlockSpec((rows, width), lambda i: (0, 0)),
        scratch_shapes=[
            pltpu.VMEM((rows, width), jnp.float32),
            pltpu.VMEM((experts, rows), jnp.float32),
            pltpu.VMEM((experts, rows), jnp.float32),
        ],
        compiler_params=pltpu.CompilerParams(vmem_limit_bytes=32 << 20),
        cost_estimate=pl.CostEstimate(
            flops=4 * experts * most * rows * width,
            bytes_accessed=2 * (experts * most + rows) * width,
            transcendentals=0,
        ),
        name="combine",
    )(ids_t, gates_t, returned)


def body(tokens, expert_ids, route_gates, expert_weights):
    groups = lax.axis_size("expert")
    experts = expert_weights.shape[0] * groups
    model = tokens.shape[1]
    ids_t = expert_ids.T
    gates_t = route_gates.T
    weights = lax.all_to_all(expert_weights, "tensor", split_axis=0, concat_axis=0, tiled=True)
    outgoing = dispatch(ids_t, tokens, experts)
    arrived = lax.all_to_all(outgoing, AXES, split_axis=0, concat_axis=0, tiled=True)
    outputs = expert_ffn(arrived.reshape(experts * MOST, model), weights)
    returned = lax.all_to_all(
        outputs.reshape(experts, MOST, model), AXES, split_axis=0, concat_axis=0, tiled=True
    )
    return combine(ids_t, gates_t, returned)


def solution(mesh):
    in_specs = (
        P(AXES, None),
        P(AXES, None),
        P(AXES, None),
        P("expert", None, "tensor", None),
    )
    return jax.shard_map(
        body, mesh=mesh, in_specs=in_specs, out_specs=P(AXES, None), check_vma=False
    )
```

time: 1090 us -> 370 us (0.34)
  waiting for transfers between devices: 355 us -> 0 us
  matrix products: 242 us -> 0 us
  local copies, waits for them, and re-layouts: 165 us -> 1.75 us
  blocking collectives: 197 us -> 332 us
  other arithmetic: 80.5 us -> 0.01 us
  starting transfers between devices: 41.2 us -> 0 us
  Pallas kernels: 0 us -> 34.9 us
    all_to_all x3 -> x0, waiting for transfers between devices: 355 us -> none  [the longest x1 156 us: body(): lax.all_to_all(expert_weights, 'tensor', split_axis=0, concat_axis=2, til...]
    dot_general x18 -> x0, matrix products: 242 us -> none  [the longest x16 220 us: add_block(): jnp.einsum('ehr,ehd->erd', hidden_part, down_part, preferred_element_type...]
    all_to_all x2 -> x3, blocking collectives: 197 us -> 332 us  [the longest x1 112 us: body(): lax.all_to_all(outputs.reshape(experts, MOST, model), AXES, split_axis=0,...]
    unnamed x2 -> x1, other arithmetic: 51.1 us -> 0.01 us
    convert_element_type x1 -> x0, local copies, waits for them, and re-layouts: 48.4 us -> none  [expert_block(): return total.astype(jnp.bfloat16)]
    unnamed x18 -> x14, local copies, waits for them, and re-layouts: 46.4 us -> 1.75 us
    all_to_all x3 -> x0, starting transfers between devices: 41.2 us -> none  [the longest x1 23.2 us: body(): lax.all_to_all(results, 'expert', split_axis=1, concat_axis=0, tiled=True)]
    all_to_all x4 -> x0, local copies, waits for them, and re-layouts: 40.9 us -> none  [the longest x1 12.1 us: body(): lax.all_to_all(results, 'expert', split_axis=1, concat_axis=0, tiled=True)]
  transfers between devices with their start and end apart: 3 -> 0, of which waited for: 3 -> 0; matrix products, arithmetic and copies ran while one was open for 2% -> 0% of each run, Pallas kernels for 0% -> 0%
where the time goes in v1:
time: 370 us; the launch traced here: 369 us
  blocking collectives  332 us (90%)
  Pallas kernels  34.9 us (9%)
    all_to_all x1, blocking collectives, body(): lax.all_to_all(outputs.reshape(experts, MOST, model), AXES, split_axis=0,...  112 us
    all_to_all x1, blocking collectives, body(): lax.all_to_all(expert_weights, 'tensor', split_axis=0, concat_axis=0, til...  110 us
    all_to_all x1, blocking collectives, body(): lax.all_to_all(outgoing, AXES, split_axis=0, concat_axis=0, tiled=True)  110 us
    pallas_call x1, Pallas kernels, expert_ffn(): pl.pallas_call(ffn_kernel, out_shape=jax.ShapeDtypeStruct((count, model),...  26.3 us

profile of v1, /device:TPU:6, one launch (start us, length us, event | category | flops | bytes accessed | tf_op | source)
XLA Modules:
  0.0 369.0 jit_solution(13318142161911395870)
XLA Ops:
  0.0 0.0 copy-start
  0.0 1.0 copy-done
  1.0 0.0 copy-start.1
  1.0 0.7 copy-done.1
  1.7 0.0 slice-start
  1.7 0.0 slice-start.1
  1.7 3.6 dispatch.1
  5.4 0.0 slice-start.2
  5.4 110.1 %all_to_all.15 = bf16[128,16,2048]{2,1,0:T(8,128)(2,1)} all-to-all(bf16[128,16,2048]{2,1,0:T(8,128)(2,1)S(1)} %dispatch.1), channel_id=1, replica_groups=mesh['expert'=8,'tensor'=16] {'expert','tensor'}, dimensions={0} | all-to-all | bytes 16777216 | tf_op jit(solution)/shard_map/all_to_all | solution.py:179
  115.5 0.0 slice-done
  115.5 0.0 slice-done.1
  115.5 0.0 slice-done.2
  115.5 110.1 %all_to_all.16.weights_ref = bf16[16,3,48,2048]{3,2,1,0:T(8,128)(2,1)} all-to-all(bf16[16,3,48,2048]{3,2,1,0:T(8,128)(2,1)S(1)} %bitcast.8), channel_id=1, replica_groups=mesh['expert'=8,'tensor'=16] {'tensor'}, dimensions={0} | all-to-all | bytes 18874368 | tf_op jit(solution)/shard_map/all_to_all | solution.py:177
  225.6 26.3 %expert_ffn.1 = bf16[2048,2048]{1,0:T(8,128)(2,1)} custom-call(bf16[2048,2048]{1,0:T(8,128)(2,1)} %bitcast.9, bf16[16,3,48,2048]{3,2,1,0:T(8,128)(2,1)} %all_to_all.16.weights_ref), custom_call_target="tpu_custom_call" | custom-call | flops 19327352832 | bytes 26214400 | tf_op jit(solution)/shard_map/expert_ffn/pallas_call | solution.py:86
  251.9 0.0 copy-start.2
  252.0 0.0 copy-start.3
  252.0 112.0 %all_to_all.17.rows_ref = bf16[128,16,2048]{2,1,0:T(8,128)(2,1)S(1)} all-to-all(bf16[128,16,2048]{2,1,0:T(8,128)(2,1)} %bitcast.10), channel_id=1, replica_groups=mesh['expert'=8,'tensor'=16] {'expert','tensor'}, dimensions={0} | all-to-all | bytes 16777216 | tf_op jit(solution)/shard_map/all_to_all | solution.py:181
  364.0 0.0 copy-done.2
  364.0 0.0 copy-done.3
  364.0 5.0 %combine.1 = bf16[128,2048]{1,0:T(8,128)(2,1)} custom-call(s32[8,128]{1,0:T(8,128)S(1)} %bitcast.5, f32[8,128]{1,0:T(8,128)S(1)} %bitcast.6, bf16[128,16,2048]{2,1,0:T(8,128)(2,1)S(1)} %all_to_all.17.rows_ref), custom_call_target="tpu_custom_call" | custom-call | flops 2147483648 | bytes 8912896 | tf_op jit(solution)/shard_map/combine/pallas_call | solution.py:146
  (1 shorter events, 0.0 us)
Async XLA Ops:
  0.0 1.0 copy-start
  1.0 0.7 copy-start.1
  1.7 113.7 %slice-start = ((s8[9437184]{0:T(1024)(128)(4,1)}), s8[4194304]{0:T(1024)(128)(4,1)S(1)}, s32[]{:S(2)}) async-start(s8[9437184]{0:T(1024)(128)(4,1)} %bitcast.7), calls=%async_computation.3 | async-start | bytes 8388608
  1.7 113.7 %slice-start.1 = ((s8[9437184]{0:T(1024)(128)(4,1)}), s8[4194304]{0:T(1024)(128)(4,1)S(1)}, s32[]{:S(2)}) async-start(s8[9437184]{0:T(1024)(128)(4,1)} %bitcast.7), calls=%async_computation.4 | async-start | bytes 8388608
  5.4 110.1 %slice-start.2 = ((s8[9437184]{0:T(1024)(128)(4,1)}), s8[1048576]{0:T(1024)(128)(4,1)S(1)}, s32[]{:S(2)}) async-start(s8[9437184]{0:T(1024)(128)(4,1)} %bitcast.7), calls=%async_computation.5 | async-start | bytes 2097152
  251.9 112.0 %copy-start.2 = (s32[128,8]{0,1:T(8,128)S(1)}, s32[128,8]{0,1:T(8,128)}, u32[]{:S(2)}) copy-start(s32[128,8]{0,1:T(8,128)} %param.5) | copy-start | bytes 12292
  252.0 112.0 %copy-start.3 = (f32[128,8]{0,1:T(8,128)S(1)}, f32[128,8]{0,1:T(8,128)}, u32[]{:S(2)}) copy-start(f32[128,8]{0,1:T(8,128)} %param.6) | copy-start | bytes 12292

commit v2 on v1

--- a/solution.py
+++ b/solution.py
@@ -1,3 +1,5 @@
+import functools
+
 import jax
 import jax.numpy as jnp
 from jax import lax
@@ -26,8 +28,10 @@
     return jnp.where(member, rank, -1.0)
 
 
-def dispatch_kernel(ids_ref, tokens_ref, out_ref, code_ref):
-    part = out_ref.shape[0]
+def dispatch_kernel(ids_ref, tokens_ref, *refs):
+    code_ref = refs[-1]
+    out_refs = refs[:-1]
+    part = out_refs[0].shape[0]
     step = pl.program_id(0)
 
     @pl.when(step == 0)
@@ -36,25 +40,29 @@
 
     code = code_ref[pl.ds(pl.multiple_of(step * part, part), part), :]
     rows = code.shape[1]
-    slots = lax.broadcasted_iota(jnp.int32, (part, MOST, rows), 1).astype(jnp.float32)
-    pick = jnp.where(code[:, None, :] == slots, 1.0, 0.0)
-    pick = pick.reshape(part * MOST, rows).astype(jnp.bfloat16)
-    picked = jnp.dot(pick, tokens_ref[...], preferred_element_type=jnp.float32)
-    out_ref[...] = picked.astype(jnp.bfloat16).reshape(out_ref.shape)
-
-
-def dispatch(ids_t, tokens, experts):
+    first = 0
+    for out_ref in out_refs:
+        count = out_ref.shape[1]
+        slots = first + lax.broadcasted_iota(jnp.int32, (part, count, rows), 1)
+        pick = jnp.where(code[:, None, :] == slots.astype(jnp.float32), 1.0, 0.0)
+        pick = pick.reshape(part * count, rows).astype(jnp.bfloat16)
+        picked = jnp.dot(pick, tokens_ref[...], preferred_element_type=jnp.float32)
+        out_ref[...] = picked.reshape(out_ref.shape).astype(jnp.bfloat16)
+        first += count
+
+
+def dispatch(ids_t, tokens, experts, counts):
     rows, width = tokens.shape
     part = 16
     return pl.pallas_call(
         dispatch_kernel,
-        out_shape=jax.ShapeDtypeStruct((experts, MOST, width), jnp.bfloat16),
+        out_shape=[jax.ShapeDtypeStruct((experts, n, width), jnp.bfloat16) for n in counts],
         grid=(experts // part,),
         in_specs=[
             pl.BlockSpec(ids_t.shape, lambda i: (0, 0)),
             pl.BlockSpec((rows, width), lambda i: (0, 0)),
         ],
-        out_specs=pl.BlockSpec((part, MOST, width), lambda i: (i, 0, 0)),
+        out_specs=[pl.BlockSpec((part, n, width), lambda i: (i, 0, 0)) for n in counts],
         scratch_shapes=[pltpu.VMEM((experts, rows), jnp.float32)],
         compiler_params=pltpu.CompilerParams(vmem_limit_bytes=32 << 20),
         cost_estimate=pl.CostEstimate(
@@ -102,8 +110,9 @@
     )(rows, weights)
 
 
-def combine_kernel(ids_ref, gates_ref, rows_ref, out_ref, total_ref, code_ref, gate_ref):
-    part = rows_ref.shape[0]
+def combine_kernel(first, ids_ref, gates_ref, rows_ref, *refs):
+    *start_refs, out_ref, total_ref, code_ref, gate_ref = refs
+    part, count, width = rows_ref.shape
     step = pl.program_id(0)
 
     @pl.when(step == 0)
@@ -116,19 +125,19 @@
         for k in range(ids_t.shape[0]):
             gate = jnp.where(names == ids_t[k : k + 1, :], gates_ref[k : k + 1, :], gate)
         gate_ref[...] = gate
-        total_ref[...] = jnp.zeros_like(total_ref)
+        total_ref[...] = start_refs[0][...] if start_refs else jnp.zeros_like(total_ref)
 
     here = pl.ds(pl.multiple_of(step * part, part), part)
     code = code_ref[here, :]
     gate = gate_ref[here, :]
     rows = code.shape[1]
-    slots = lax.broadcasted_iota(jnp.int32, (part, MOST, rows), 1).astype(jnp.float32)
-    weight = jnp.where(code[:, None, :] == slots, gate[:, None, :], 0.0)
-    weight = weight.reshape(part * MOST, rows)
+    slots = first + lax.broadcasted_iota(jnp.int32, (part, count, rows), 1)
+    weight = jnp.where(code[:, None, :] == slots.astype(jnp.float32), gate[:, None, :], 0.0)
+    weight = weight.reshape(part * count, rows)
     high = weight.astype(jnp.bfloat16)
     low = (weight - high.astype(jnp.float32)).astype(jnp.bfloat16)
     both = jnp.concatenate([high, low], axis=1)
-    values = rows_ref[...].reshape(part * MOST, rows_ref.shape[2])
+    values = rows_ref[...].reshape(part * count, width)
     sums = lax.dot_general(
         both, values, (((0,), (0,)), ((), ())), preferred_element_type=jnp.float32
     )
@@ -136,23 +145,25 @@
 
     @pl.when(step == pl.num_programs(0) - 1)
     def _():
-        out_ref[...] = total_ref[...].astype(jnp.bfloat16)
-
-
-def combine(ids_t, gates_t, returned):
-    experts, most, width = returned.shape
+        out_ref[...] = total_ref[...].astype(out_ref.dtype)
+
+
+def combine(ids_t, gates_t, returned, first, start, dtype):
+    experts, count, width = returned.shape
     rows = ids_t.shape[1]
     part = 16
+    whole = pl.BlockSpec((rows, width), lambda i: (0, 0))
     return pl.pallas_call(
-        combine_kernel,
-        out_shape=jax.ShapeDtypeStruct((rows, width), jnp.bfloat16),
+        functools.partial(combine_kernel, first),
+        out_shape=jax.ShapeDtypeStruct((rows, width), dtype),
         grid=(experts // part,),
         in_specs=[
             pl.BlockSpec(ids_t.shape, lambda i: (0, 0)),
             pl.BlockSpec(gates_t.shape, lambda i: (0, 0)),
-            pl.BlockSpec((part, most, width), lambda i: (i, 0, 0)),
-        ],
-        out_specs=pl.BlockSpec((rows, width), lambda i: (0, 0)),
+            pl.BlockSpec((part, count, width), lambda i: (i, 0, 0)),
+        ]
+        + [whole] * len(start),
+        out_specs=whole,
         scratch_shapes=[
             pltpu.VMEM((rows, width), jnp.float32),
             pltpu.VMEM((experts, rows), jnp.float32),
@@ -160,12 +171,16 @@
         ],
         compiler_params=pltpu.CompilerParams(vmem_limit_bytes=32 << 20),
         cost_estimate=pl.CostEstimate(
-            flops=4 * experts * most * rows * width,
-            bytes_accessed=2 * (experts * most + rows) * width,
+            flops=4 * experts * count * rows * width,
+            bytes_accessed=2 * (experts * count + rows) * width,
             transcendentals=0,
         ),
         name="combine",
-    )(ids_t, gates_t, returned)
+    )(ids_t, gates_t, returned, *start)
+
+
+def exchange(rows):
+    return lax.all_to_all(rows, AXES, split_axis=0, concat_axis=0, tiled=True)
 
 
 def body(tokens, expert_ids, route_gates, expert_weights):
@@ -174,14 +189,21 @@
     model = tokens.shape[1]
     ids_t = expert_ids.T
     gates_t = route_gates.T
+    half = MOST // 2
     weights = lax.all_to_all(expert_weights, "tensor", split_axis=0, concat_axis=0, tiled=True)
-    outgoing = dispatch(ids_t, tokens, experts)
-    arrived = lax.all_to_all(outgoing, AXES, split_axis=0, concat_axis=0, tiled=True)
-    outputs = expert_ffn(arrived.reshape(experts * MOST, model), weights)
-    returned = lax.all_to_all(
-        outputs.reshape(experts, MOST, model), AXES, split_axis=0, concat_axis=0, tiled=True
-    )
-    return combine(ids_t, gates_t, returned)
+    out_a, out_b = dispatch(ids_t, tokens, experts, (half, half))
+    out_a, out_b, weights = lax.optimization_barrier((out_a, out_b, weights))
+    in_a = exchange(out_a)
+    in_a, out_b = lax.optimization_barrier((in_a, out_b))
+    in_b = exchange(out_b)
+    done_a = expert_ffn(in_a.reshape(experts * half, model), weights)
+    done_a, in_b = lax.optimization_barrier((done_a, in_b))
+    back_a = exchange(done_a.reshape(experts, half, model))
+    done_b = expert_ffn(in_b.reshape(experts * half, model), weights)
+    done_b, back_a = lax.optimization_barrier((done_b, back_a))
+    back_b = exchange(done_b.reshape(experts, half, model))
+    part = combine(ids_t, gates_t, back_a, 0, (), jnp.float32)
+    return combine(ids_t, gates_t, back_b, half, (part,), jnp.bfloat16)
 
 
 def solution(mesh):

time: 370 us -> 423 us (1.14)
  waiting for transfers between devices: 0 us -> 275 us
  blocking collectives: 332 us -> 68.1 us
  starting transfers between devices: 0 us -> 23 us
  Pallas kernels: 34.9 us -> 47.7 us
  local copies, waits for them, and re-layouts: 1.75 us -> 8 us
    all_to_all x0 -> x4, waiting for transfers between devices: none -> 275 us  [the longest x1 156 us: body(): lax.all_to_all(expert_weights, 'tensor', split_axis=0, concat_axis=0, til...]
    all_to_all x3 -> x1, blocking collectives: 332 us -> 68.1 us  [exchange(): return lax.all_to_all(rows, AXES, split_axis=0, concat_axis=0, tiled=True)]
    all_to_all x0 -> x4, starting transfers between devices: none -> 23 us  [the longest x3 14.7 us: exchange(): return lax.all_to_all(rows, AXES, split_axis=0, concat_axis=0, tiled=True)]
    pallas_call x2 -> x3, Pallas kernels: 8.61 us -> 18.4 us  [the longest x2 14.7 us: combine(): pl.pallas_call(functools.partial(combine_kernel, first), out_shape=jax.Sh...]
    unnamed x14, local copies, waits for them, and re-layouts: 1.75 us -> 8 us
    pallas_call x1 -> x2, Pallas kernels: 26.3 us -> 29.3 us  [expert_ffn(): pl.pallas_call(ffn_kernel, out_shape=jax.ShapeDtypeStruct((count, model),...]
  transfers between devices with their start and end apart: 0 -> 4, of which waited for: 0 -> 4; matrix products, arithmetic and copies ran while one was open for 0% -> 0% of each run, Pallas kernels for 0% -> 9%
where the time goes in v2:
time: 423 us; the launch traced here: 422 us
  waiting for transfers between devices  275 us (65%)
  blocking collectives  68.1 us (16%)
  Pallas kernels  47.7 us (11%)
  starting transfers between devices  23 us (5%)
  local copies, waits for them, and re-layouts  8 us (2%)
    all_to_all x1, waiting for transfers between devices, body(): lax.all_to_all(expert_weights, 'tensor', split_axis=0, concat_axis=0, til...  156 us
    all_to_all x3, waiting for transfers between devices, exchange(): return lax.all_to_all(rows, AXES, split_axis=0, concat_axis=0, tiled=True)  119 us
    all_to_all x1, blocking collectives, exchange(): return lax.all_to_all(rows, AXES, split_axis=0, concat_axis=0, tiled=True)  68.1 us
    pallas_call x2, Pallas kernels, expert_ffn(): pl.pallas_call(ffn_kernel, out_shape=jax.ShapeDtypeStruct((count, model),...  29.3 us
    all_to_all x3, starting transfers between devices, exchange(): return lax.all_to_all(rows, AXES, split_axis=0, concat_axis=0, tiled=True)  14.7 us
    pallas_call x2, Pallas kernels, combine(): pl.pallas_call(functools.partial(combine_kernel, first), out_shape=jax.Sh...  14.7 us
  transfers between devices with their start and end apart: 4, of which 4 were waited for; matrix products, arithmetic and copies ran while one was open for 0% of the time, Pallas kernels for 9%

profile of v2, /device:TPU:6, one launch (start us, length us, event | category | flops | bytes accessed | tf_op | source)
XLA Modules:
  0.0 422.3 jit_solution(14002197884598374720)
XLA Ops:
  0.0 0.0 copy-start.4
  0.0 0.0 copy-start.6
  0.0 8.2 %all-to-all-start = ((bf16[16,3,48,2048]{3,2,1,0:T(8,128)(2,1)}), bf16[16,3,48,2048]{3,2,1,0:T(8,128)(2,1)}, u32[]{:S(2)}, u32[]{:S(2)}) async-start(bf16[16,3,48,2048]{3,2,1,0:T(8,128)(2,1)} %param.7), calls=%async_computation | async-start | bytes 18874368 | tf_op jit(solution)/shard_map/all_to_all | solution.py:193
  8.2 0.0 copy-done.4
  8.2 0.0 copy-done.6
  8.3 3.7 dispatch.1
  11.9 0.0 copy-start
  11.9 2.1 copy-done
  14.0 0.0 copy-start.3
  14.0 2.0 copy-done.3
  16.0 156.4 %all-to-all-done.weights_ref = bf16[16,3,48,2048]{3,2,1,0:T(8,128)(2,1)} async-done(((bf16[16,3,48,2048]{3,2,1,0:T(8,128)(2,1)}), bf16[16,3,48,2048]{3,2,1,0:T(8,128)(2,1)}, u32[]{:S(2)}, u32[]{:S(2)}) %all-to-all-start) | async-done | bytes 9437216 | tf_op jit(solution)/shard_map/all_to_all | solution.py:193
  172.4 68.1 %all_to_all.25 = bf16[128,8,2048]{2,1,0:T(8,128)(2,1)} all-to-all(bf16[128,8,2048]{2,1,0:T(8,128)(2,1)} %copy-done.3), channel_id=1, replica_groups=mesh['expert'=8,'tensor'=16] {'expert','tensor'}, dimensions={0} | all-to-all | bytes 8388608 | tf_op jit(solution)/shard_map/all_to_all | solution.py:183
  240.5 4.9 %all-to-all-start.2 = ((bf16[128,8,2048]{2,1,0:T(8,128)(2,1)}), bf16[128,8,2048]{2,1,0:T(8,128)(2,1)}, u32[]{:S(2)}, u32[]{:S(2)}) async-start(bf16[128,8,2048]{2,1,0:T(8,128)(2,1)} %copy-done), calls=%async_computation.2 | async-start | bytes 8388608 | tf_op jit(solution)/shard_map/all_to_all | solution.py:183
  245.4 14.7 %expert_ffn.2 = bf16[1024,2048]{1,0:T(8,128)(2,1)S(1)} custom-call(bf16[1024,2048]{1,0:T(8,128)(2,1)} %bitcast.13, bf16[16,3,48,2048]{3,2,1,0:T(8,128)(2,1)} %all-to-all-done.weights_ref), custom_call_target="tpu_custom_call" | custom-call | flops 9663676416 | bytes 17825792 | tf_op jit(solution)/shard_map/expert_ffn/pallas_call | solution.py:94
  260.1 0.0 copy-start.1
  260.1 2.0 copy-done.1
  262.1 36.4 %all-to-all-done.2 = bf16[128,8,2048]{2,1,0:T(8,128)(2,1)} async-done(((bf16[128,8,2048]{2,1,0:T(8,128)(2,1)}), bf16[128,8,2048]{2,1,0:T(8,128)(2,1)}, u32[]{:S(2)}, u32[]{:S(2)}) %all-to-all-start.2) | async-done | bytes 4194336 | tf_op jit(solution)/shard_map/all_to_all | solution.py:183
  298.5 4.9 %all-to-all-start.3 = ((bf16[128,8,2048]{2,1,0:T(8,128)(2,1)}), bf16[128,8,2048]{2,1,0:T(8,128)(2,1)}, u32[]{:S(2)}, u32[]{:S(2)}) async-start(bf16[128,8,2048]{2,1,0:T(8,128)(2,1)} %bitcast.6), calls=%async_computation.3 | async-start | bytes 8388608 | tf_op jit(solution)/shard_map/all_to_all | solution.py:183
  303.4 14.7 %expert_ffn.3 = bf16[1024,2048]{1,0:T(8,128)(2,1)S(1)} custom-call(bf16[1024,2048]{1,0:T(8,128)(2,1)} %bitcast.3.rows_ref, bf16[16,3,48,2048]{3,2,1,0:T(8,128)(2,1)} %all-to-all-done.weights_ref), custom_call_target="tpu_custom_call" | custom-call | flops 9663676416 | bytes 17825792 | tf_op jit(solution)/shard_map/expert_ffn/pallas_call | solution.py:94
  318.1 0.0 copy-start.2
  318.1 1.9 copy-done.2
  320.0 36.5 %all-to-all-done.3.rows_ref = bf16[128,8,2048]{2,1,0:T(8,128)(2,1)} async-done(((bf16[128,8,2048]{2,1,0:T(8,128)(2,1)}), bf16[128,8,2048]{2,1,0:T(8,128)(2,1)}, u32[]{:S(2)}, u32[]{:S(2)}) %all-to-all-start.3) | async-done | bytes 4194336 | tf_op jit(solution)/shard_map/all_to_all | solution.py:183
  356.5 0.0 copy-start.5
  356.5 4.9 %all-to-all-start.4 = ((bf16[128,8,2048]{2,1,0:T(8,128)(2,1)}), bf16[128,8,2048]{2,1,0:T(8,128)(2,1)}, u32[]{:S(2)}, u32[]{:S(2)}) async-start(bf16[128,8,2048]{2,1,0:T(8,128)(2,1)} %bitcast.7), calls=%async_computation.4 | async-start | bytes 8388608 | tf_op jit(solution)/shard_map/all_to_all | solution.py:183
  361.4 0.0 copy-done.5
  361.4 7.0 %combine.2.refs_0_ = f32[128,2048]{1,0:T(8,128)S(1)} custom-call(s32[8,128]{1,0:T(8,128)S(1)} %bitcast.9, f32[8,128]{1,0:T(8,128)S(1)} %bitcast.11, bf16[128,8,2048]{2,1,0:T(8,128)(2,1)} %all-to-all-done.3.rows_ref), custom_call_target="tpu_custom_call" | custom-call | flops 1073741824 | bytes 4718592 | tf_op jit(solution)/shard_map/combine/pallas_call | solution.py:156
  368.5 46.1 %all-to-all-done.4.rows_ref = bf16[128,8,2048]{2,1,0:T(8,128)(2,1)} async-done(((bf16[128,8,2048]{2,1,0:T(8,128)(2,1)}), bf16[128,8,2048]{2,1,0:T(8,128)(2,1)}, u32[]{:S(2)}, u32[]{:S(2)}) %all-to-all-start.4) | async-done | bytes 4194336 | tf_op jit(solution)/shard_map/all_to_all | solution.py:183
  414.6 7.7 %combine.3 = bf16[128,2048]{1,0:T(8,128)(2,1)} custom-call(s32[8,128]{1,0:T(8,128)S(1)} %bitcast.10, f32[8,128]{1,0:T(8,128)S(1)} %bitcast.12, bf16[128,8,2048]{2,1,0:T(8,128)(2,1)} %all-to-all-done.4.rows_ref, f32[128,2048]{1,0:T(8,128)S(1)} %combine.2.refs_0_), custom_call_target="tpu_custom_call" | custom-call | flops 1073741824 | bytes 4718592 | tf_op jit(solution)/shard_map/combine/pallas_call | solution.py:156
Async XLA Ops:
  0.0 8.2 %copy-start.4 = (s32[128,8]{0,1:T(8,128)S(1)}, s32[128,8]{0,1:T(8,128)}, u32[]{:S(2)}) copy-start(s32[128,8]{0,1:T(8,128)} %param.5) | copy-start | bytes 12292
  0.0 8.2 %copy-start.6 = (bf16[128,2048]{1,0:T(8,128)(2,1)S(1)}, bf16[128,2048]{1,0:T(8,128)(2,1)}, u32[]{:S(2)}) copy-start(bf16[128,2048]{1,0:T(8,128)(2,1)} %tokens_ref.1) | copy-start | bytes 1572868
  0.0 172.4 %all-to-all-start = ((bf16[16,3,48,2048]{3,2,1,0:T(8,128)(2,1)}), bf16[16,3,48,2048]{3,2,1,0:T(8,128)(2,1)}, u32[]{:S(2)}, u32[]{:S(2)}) async-start(bf16[16,3,48,2048]{3,2,1,0:T(8,128)(2,1)} %param.7), calls=%async_computation | async-start | bytes 18874368 | tf_op jit(solution)/shard_map/all_to_all | solution.py:193
  11.9 2.1 copy-start
  14.0 2.0 copy-start.3
  240.5 58.0 %all-to-all-start.2 = ((bf16[128,8,2048]{2,1,0:T(8,128)(2,1)}), bf16[128,8,2048]{2,1,0:T(8,128)(2,1)}, u32[]{:S(2)}, u32[]{:S(2)}) async-start(bf16[128,8,2048]{2,1,0:T(8,128)(2,1)} %copy-done), calls=%async_computation.2 | async-start | bytes 8388608 | tf_op jit(solution)/shard_map/all_to_all | solution.py:183
  260.1 2.0 copy-start.1
  298.5 58.0 %all-to-all-start.3 = ((bf16[128,8,2048]{2,1,0:T(8,128)(2,1)}), bf16[128,8,2048]{2,1,0:T(8,128)(2,1)}, u32[]{:S(2)}, u32[]{:S(2)}) async-start(bf16[128,8,2048]{2,1,0:T(8,128)(2,1)} %bitcast.6), calls=%async_computation.3 | async-start | bytes 8388608 | tf_op jit(solution)/shard_map/all_to_all | solution.py:183
  318.1 2.0 copy-start.2
  356.5 4.9 %copy-start.5 = (f32[128,8]{0,1:T(8,128)S(1)}, f32[128,8]{0,1:T(8,128)}, u32[]{:S(2)}) copy-start(f32[128,8]{0,1:T(8,128)} %param.6) | copy-start | bytes 12292
  356.5 58.1 %all-to-all-start.4 = ((bf16[128,8,2048]{2,1,0:T(8,128)(2,1)}), bf16[128,8,2048]{2,1,0:T(8,128)(2,1)}, u32[]{:S(2)}, u32[]{:S(2)}) async-start(bf16[128,8,2048]{2,1,0:T(8,128)(2,1)} %bitcast.7), calls=%async_computation.4 | async-start | bytes 8388608 | tf_op jit(solution)/shard_map/all_to_all | solution.py:183

commit v3 on v2

--- a/solution.py
+++ b/solution.py
@@ -190,8 +190,9 @@
     ids_t = expert_ids.T
     gates_t = route_gates.T
     half = MOST // 2
+    out_a, out_b = dispatch(ids_t, tokens, experts, (half, half))
+    out_a, out_b, expert_weights = lax.optimization_barrier((out_a, out_b, expert_weights))
     weights = lax.all_to_all(expert_weights, "tensor", split_axis=0, concat_axis=0, tiled=True)
-    out_a, out_b = dispatch(ids_t, tokens, experts, (half, half))
     out_a, out_b, weights = lax.optimization_barrier((out_a, out_b, weights))
     in_a = exchange(out_a)
     in_a, out_b = lax.optimization_barrier((in_a, out_b))

time: 423 us -> 364 us (0.86)
  waiting for transfers between devices: 275 us -> 119 us
  blocking collectives: 68.1 us -> 176 us
  starting transfers between devices: 23 us -> 14.7 us
    all_to_all x1 -> x0, waiting for transfers between devices: 156 us -> none  [body(): lax.all_to_all(expert_weights, 'tensor', split_axis=0, concat_axis=0, til...]
    all_to_all x0 -> x1, blocking collectives: none -> 116 us  [body(): lax.all_to_all(expert_weights, 'tensor', split_axis=0, concat_axis=0, til...]
    all_to_all x1 -> x0, starting transfers between devices: 8.22 us -> none  [body(): lax.all_to_all(expert_weights, 'tensor', split_axis=0, concat_axis=0, til...]
    all_to_all x1, blocking collectives: 68.1 us -> 60 us  [exchange(): return lax.all_to_all(rows, AXES, split_axis=0, concat_axis=0, tiled=True)]
  transfers between devices with their start and end apart: 4 -> 3, of which waited for: 4 -> 3; matrix products, arithmetic and copies ran while one was open for 0% -> 0% of each run, Pallas kernels for 9% -> 10%
where the time goes in v3:
time: 364 us; the launch traced here: 363 us
  blocking collectives  176 us (48%)
  waiting for transfers between devices  119 us (33%)
  Pallas kernels  47.7 us (13%)
  starting transfers between devices  14.7 us (4%)
  local copies, waits for them, and re-layouts  5.66 us (2%)
    all_to_all x3, waiting for transfers between devices, exchange(): return lax.all_to_all(rows, AXES, split_axis=0, concat_axis=0, tiled=True)  119 us
    all_to_all x1, blocking collectives, body(): lax.all_to_all(expert_weights, 'tensor', split_axis=0, concat_axis=0, til...  116 us
    all_to_all x1, blocking collectives, exchange(): return lax.all_to_all(rows, AXES, split_axis=0, concat_axis=0, tiled=True)  60 us
    pallas_call x2, Pallas kernels, expert_ffn(): pl.pallas_call(ffn_kernel, out_shape=jax.ShapeDtypeStruct((count, model),...  29.3 us
    all_to_all x3, starting transfers between devices, exchange(): return lax.all_to_all(rows, AXES, split_axis=0, concat_axis=0, tiled=True)  14.7 us
    pallas_call x2, Pallas kernels, combine(): pl.pallas_call(functools.partial(combine_kernel, first), out_shape=jax.Sh...  14.7 us
  transfers between devices with their start and end apart: 3, of which 3 were waited for; matrix products, arithmetic and copies ran while one was open for 0% of the time, Pallas kernels for 10%

profile of v3, /device:TPU:6, one launch (start us, length us, event | category | flops | bytes accessed | tf_op | source)
XLA Modules:
  0.0 363.0 jit_solution(13377961743265210408)
XLA Ops:
  0.0 0.0 copy-start.3
  0.0 0.7 copy-done.3
  0.7 0.0 copy-start.6
  0.7 1.0 copy-done.6
  1.7 3.6 %dispatch.1 = (bf16[128,8,2048]{2,1,0:T(8,128)(2,1)S(1)}, bf16[128,8,2048]{2,1,0:T(8,128)(2,1)S(1)}) custom-call(s32[8,128]{1,0:T(8,128)S(1)} %bitcast.8, bf16[128,2048]{1,0:T(8,128)(2,1)S(1)} %copy-done.6), custom_call_target="tpu_custom_call" | custom-call | flops 1073741824 | bytes 8912896 | tf_op jit(solution)/shard_map/dispatch/pallas_call | solution.py:57
  5.4 0.0 copy-start.2
  5.4 115.9 %all_to_all.25.weights_ref = bf16[16,3,48,2048]{3,2,1,0:T(8,128)(2,1)} all-to-all(bf16[16,3,48,2048]{3,2,1,0:T(8,128)(2,1)} %param.7), channel_id=1, replica_groups=mesh['expert'=8,'tensor'=16] {'tensor'}, dimensions={0} | all-to-all | bytes 18874368 | tf_op jit(solution)/shard_map/all_to_all | solution.py:195
  121.3 0.0 copy-done.2
  121.3 60.0 %all_to_all.26 = bf16[128,8,2048]{2,1,0:T(8,128)(2,1)} all-to-all(bf16[128,8,2048]{2,1,0:T(8,128)(2,1)S(1)} %get-tuple-element.24), channel_id=1, replica_groups=mesh['expert'=8,'tensor'=16] {'expert','tensor'}, dimensions={0} | all-to-all | bytes 8388608 | tf_op jit(solution)/shard_map/all_to_all | solution.py:183
  181.3 4.9 %all-to-all-start.2 = ((bf16[128,8,2048]{2,1,0:T(8,128)(2,1)}), bf16[128,8,2048]{2,1,0:T(8,128)(2,1)}, u32[]{:S(2)}, u32[]{:S(2)}) async-start(bf16[128,8,2048]{2,1,0:T(8,128)(2,1)} %copy-done.2), calls=%async_computation.2 | async-start | bytes 8388608 | tf_op jit(solution)/shard_map/all_to_all | solution.py:183
  186.2 14.7 %expert_ffn.2 = bf16[1024,2048]{1,0:T(8,128)(2,1)S(1)} custom-call(bf16[1024,2048]{1,0:T(8,128)(2,1)} %bitcast.13, bf16[16,3,48,2048]{3,2,1,0:T(8,128)(2,1)} %all_to_all.25.weights_ref), custom_call_target="tpu_custom_call" | custom-call | flops 9663676416 | bytes 17825792 | tf_op jit(solution)/shard_map/expert_ffn/pallas_call | solution.py:94
  200.8 0.0 copy-start
  200.8 2.0 copy-done
  202.8 36.4 %all-to-all-done.2 = bf16[128,8,2048]{2,1,0:T(8,128)(2,1)} async-done(((bf16[128,8,2048]{2,1,0:T(8,128)(2,1)}), bf16[128,8,2048]{2,1,0:T(8,128)(2,1)}, u32[]{:S(2)}, u32[]{:S(2)}) %all-to-all-start.2) | async-done | bytes 4194336 | tf_op jit(solution)/shard_map/all_to_all | solution.py:183
  239.2 4.9 %all-to-all-start.3 = ((bf16[128,8,2048]{2,1,0:T(8,128)(2,1)}), bf16[128,8,2048]{2,1,0:T(8,128)(2,1)}, u32[]{:S(2)}, u32[]{:S(2)}) async-start(bf16[128,8,2048]{2,1,0:T(8,128)(2,1)} %bitcast.6), calls=%async_computation.3 | async-start | bytes 8388608 | tf_op jit(solution)/shard_map/all_to_all | solution.py:183
  244.2 14.6 %expert_ffn.3 = bf16[1024,2048]{1,0:T(8,128)(2,1)S(1)} custom-call(bf16[1024,2048]{1,0:T(8,128)(2,1)} %bitcast.3.rows_ref, bf16[16,3,48,2048]{3,2,1,0:T(8,128)(2,1)} %all_to_all.25.weights_ref), custom_call_target="tpu_custom_call" | custom-call | flops 9663676416 | bytes 17825792 | tf_op jit(solution)/shard_map/expert_ffn/pallas_call | solution.py:94
  258.8 0.0 copy-start.1
  258.8 1.9 copy-done.1
  260.8 36.5 %all-to-all-done.3.rows_ref = bf16[128,8,2048]{2,1,0:T(8,128)(2,1)} async-done(((bf16[128,8,2048]{2,1,0:T(8,128)(2,1)}), bf16[128,8,2048]{2,1,0:T(8,128)(2,1)}, u32[]{:S(2)}, u32[]{:S(2)}) %all-to-all-start.3) | async-done | bytes 4194336 | tf_op jit(solution)/shard_map/all_to_all | solution.py:183
  297.2 0.0 copy-start.4
  297.2 0.0 copy-start.5
  297.2 4.9 %all-to-all-start.4 = ((bf16[128,8,2048]{2,1,0:T(8,128)(2,1)}), bf16[128,8,2048]{2,1,0:T(8,128)(2,1)}, u32[]{:S(2)}, u32[]{:S(2)}) async-start(bf16[128,8,2048]{2,1,0:T(8,128)(2,1)} %bitcast.7), calls=%async_computation.4 | async-start | bytes 8388608 | tf_op jit(solution)/shard_map/all_to_all | solution.py:183
  302.2 0.0 copy-done.4
  302.2 0.0 copy-done.5
  302.2 7.0 %combine.2.refs_0_ = f32[128,2048]{1,0:T(8,128)S(1)} custom-call(s32[8,128]{1,0:T(8,128)S(1)} %bitcast.9, f32[8,128]{1,0:T(8,128)S(1)} %bitcast.11, bf16[128,8,2048]{2,1,0:T(8,128)(2,1)} %all-to-all-done.3.rows_ref), custom_call_target="tpu_custom_call" | custom-call | flops 1073741824 | bytes 4718592 | tf_op jit(solution)/shard_map/combine/pallas_call | solution.py:156
  309.2 46.1 %all-to-all-done.4.rows_ref = bf16[128,8,2048]{2,1,0:T(8,128)(2,1)} async-done(((bf16[128,8,2048]{2,1,0:T(8,128)(2,1)}), bf16[128,8,2048]{2,1,0:T(8,128)(2,1)}, u32[]{:S(2)}, u32[]{:S(2)}) %all-to-all-start.4) | async-done | bytes 4194336 | tf_op jit(solution)/shard_map/all_to_all | solution.py:183
  355.3 7.7 %combine.3 = bf16[128,2048]{1,0:T(8,128)(2,1)} custom-call(s32[8,128]{1,0:T(8,128)S(1)} %bitcast.10, f32[8,128]{1,0:T(8,128)S(1)} %bitcast.12, bf16[128,8,2048]{2,1,0:T(8,128)(2,1)} %all-to-all-done.4.rows_ref, f32[128,2048]{1,0:T(8,128)S(1)} %combine.2.refs_0_), custom_call_target="tpu_custom_call" | custom-call | flops 1073741824 | bytes 4718592 | tf_op jit(solution)/shard_map/combine/pallas_call | solution.py:156
Async XLA Ops:
  0.0 0.7 copy-start.3
  0.7 1.0 copy-start.6
  5.4 115.9 %copy-start.2 = (bf16[128,8,2048]{2,1,0:T(8,128)(2,1)}, bf16[128,8,2048]{2,1,0:T(8,128)(2,1)S(1)}, u32[]{:S(2)}) copy-start(bf16[128,8,2048]{2,1,0:T(8,128)(2,1)S(1)} %get-tuple-element.28) | copy-start | bytes 12582916
  181.3 58.0 %all-to-all-start.2 = ((bf16[128,8,2048]{2,1,0:T(8,128)(2,1)}), bf16[128,8,2048]{2,1,0:T(8,128)(2,1)}, u32[]{:S(2)}, u32[]{:S(2)}) async-start(bf16[128,8,2048]{2,1,0:T(8,128)(2,1)} %copy-done.2), calls=%async_computation.2 | async-start | bytes 8388608 | tf_op jit(solution)/shard_map/all_to_all | solution.py:183
  200.8 2.0 copy-start
  239.2 58.0 %all-to-all-start.3 = ((bf16[128,8,2048]{2,1,0:T(8,128)(2,1)}), bf16[128,8,2048]{2,1,0:T(8,128)(2,1)}, u32[]{:S(2)}, u32[]{:S(2)}) async-start(bf16[128,8,2048]{2,1,0:T(8,128)(2,1)} %bitcast.6), calls=%async_computation.3 | async-start | bytes 8388608 | tf_op jit(solution)/shard_map/all_to_all | solution.py:183
  258.8 1.9 copy-start.1
  297.2 4.9 %copy-start.4 = (s32[128,8]{0,1:T(8,128)S(1)}, s32[128,8]{0,1:T(8,128)}, u32[]{:S(2)}) copy-start(s32[128,8]{0,1:T(8,128)} %param.5) | copy-start | bytes 12292
  297.2 4.9 %copy-start.5 = (f32[128,8]{0,1:T(8,128)S(1)}, f32[128,8]{0,1:T(8,128)}, u32[]{:S(2)}) copy-start(f32[128,8]{0,1:T(8,128)} %param.6) | copy-start | bytes 12292
  297.2 58.1 %all-to-all-start.4 = ((bf16[128,8,2048]{2,1,0:T(8,128)(2,1)}), bf16[128,8,2048]{2,1,0:T(8,128)(2,1)}, u32[]{:S(2)}, u32[]{:S(2)}) async-start(bf16[128,8,2048]{2,1,0:T(8,128)(2,1)} %bitcast.7), calls=%async_computation.4 | async-start | bytes 8388608 | tf_op jit(solution)/shard_map/all_to_all | solution.py:183

commit v4 on v1

v4 whole, which is shorter than its diff:
```python
import functools

import jax
import jax.numpy as jnp
from jax import lax
from jax.experimental import pallas as pl
from jax.experimental.pallas import tpu as pltpu
from jax.sharding import PartitionSpec as P

MOST = 16
AXES = ("expert", "tensor")


def slot_codes(ids_t, experts):
    top, rows = ids_t.shape
    names = lax.broadcasted_iota(jnp.int32, (experts, rows), 0)
    member = names == ids_t[0:1, :]
    for k in range(1, top):
        member = member | (names == ids_t[k : k + 1, :])
    before = lax.broadcasted_iota(jnp.int32, (rows, rows), 0) < lax.broadcasted_iota(
        jnp.int32, (rows, rows), 1
    )
    rank = jnp.dot(
        member.astype(jnp.float32).astype(jnp.bfloat16),
        before.astype(jnp.float32).astype(jnp.bfloat16),
        preferred_element_type=jnp.float32,
    )
    return jnp.where(member, rank, -1.0)


def dispatch_kernel(first, ids_hbm, tokens_hbm, out_ref, ids_ref, tokens_ref, code_ref, sem):
    part, count, width = out_ref.shape
    step = pl.program_id(0)

    @pl.when(step == 0)
    def _():
        load_ids = pltpu.make_async_copy(ids_hbm, ids_ref, sem.at[0])
        load_tokens = pltpu.make_async_copy(tokens_hbm, tokens_ref, sem.at[1])
        load_ids.start()
        load_tokens.start()
        load_ids.wait()
        code_ref[...] = slot_codes(ids_ref[...], code_ref.shape[0])
        load_tokens.wait()

    code = code_ref[pl.ds(pl.multiple_of(step * part, part), part), :]
    rows = code.shape[1]
    slots = first + lax.broadcasted_iota(jnp.int32, (part, count, rows), 1)
    pick = jnp.where(code[:, None, :] == slots.astype(jnp.float32), 1.0, 0.0)
    pick = pick.reshape(part * count, rows).astype(jnp.bfloat16)
    picked = jnp.dot(pick, tokens_ref[...], preferred_element_type=jnp.float32)
    out_ref[...] = picked.reshape(out_ref.shape).astype(jnp.bfloat16)


def dispatch(ids_t, tokens, experts, first, count):
    rows, width = tokens.shape
    part = 32
    return pl.pallas_call(
        functools.partial(dispatch_kernel, first),
        out_shape=pltpu.HBM((experts, count, width), jnp.bfloat16),
        grid=(experts // part,),
        in_specs=[pl.BlockSpec(memory_space=pltpu.HBM)] * 2,
        out_specs=pl.BlockSpec((part, count, width), lambda i: (i, 0, 0)),
        scratch_shapes=[
            pltpu.VMEM(ids_t.shape, ids_t.dtype),
            pltpu.VMEM((rows, width), tokens.dtype),
            pltpu.VMEM((experts, rows), jnp.float32),
            pltpu.SemaphoreType.DMA((2,)),
        ],
        compiler_params=pltpu.CompilerParams(vmem_limit_bytes=32 << 20),
        cost_estimate=pl.CostEstimate(
            flops=2 * experts * count * rows * width,
            bytes_accessed=2 * (experts * count + rows) * width,
            transcendentals=0,
        ),
        name="dispatch",
    )(
        pltpu.with_memory_space_constraint(ids_t, pltpu.HBM),
        pltpu.with_memory_space_constraint(tokens, pltpu.HBM),
    )


def ffn_kernel(rows_ref, weights_ref, out_ref):
    blocks, _, width_block, model = weights_ref.shape
    hidden_units = blocks * width_block
    contract_last = (((1,), (1,)), ((), ()))
    x = rows_ref[...]
    w_gate = weights_ref[:, 0].reshape(hidden_units, model)
    w_up = weights_ref[:, 1].reshape(hidden_units, model)
    w_down = weights_ref[:, 2].reshape(hidden_units, model)
    gate = lax.dot_general(x, w_gate, contract_last, preferred_element_type=jnp.float32)
    up = lax.dot_general(x, w_up, contract_last, preferred_element_type=jnp.float32)
    hidden = (gate / (1.0 + jnp.exp(-gate)) * up).astype(jnp.bfloat16)
    out_ref[...] = jnp.dot(hidden, w_down, preferred_element_type=jnp.float32).astype(jnp.bfloat16)


def expert_ffn(rows, weights):
    count, model = rows.shape
    part = 256
    return pl.pallas_call(
        ffn_kernel,
        out_shape=jax.ShapeDtypeStruct((count, model), jnp.bfloat16),
        grid=(count // part,),
        in_specs=[
            pl.BlockSpec((part, model), lambda i: (i, 0)),
            pl.BlockSpec(weights.shape, lambda i: (0, 0, 0, 0), pipeline_mode=pl.Buffered(1)),
        ],
        out_specs=pl.BlockSpec((part, model), lambda i: (i, 0)),
        compiler_params=pltpu.CompilerParams(vmem_limit_bytes=48 << 20),
        cost_estimate=pl.CostEstimate(
            flops=2 * count * weights.size,
            bytes_accessed=2 * (2 * rows.size + weights.size),
            transcendentals=count * weights.size // (3 * model),
        ),
        name="expert_ffn",
    )(rows, weights)


def coefficients_kernel(ids_ref, gates_ref, *out_refs):
    experts = out_refs[0].shape[1] // (MOST // len(out_refs))
    ids_t = ids_ref[...]
    rows = ids_t.shape[1]
    code = slot_codes(ids_t, experts)
    names = lax.broadcasted_iota(jnp.int32, (experts, rows), 0)
    gate = jnp.zeros((experts, rows), jnp.float32)
    for k in range(ids_t.shape[0]):
        gate = jnp.where(names == ids_t[k : k + 1, :], gates_ref[k : k + 1, :], gate)
    first = 0
    for out_ref in out_refs:
        count = out_ref.shape[1] // experts
        slots = first + lax.broadcasted_iota(jnp.int32, (experts, count, rows), 1)
        weight = jnp.where(code[:, None, :] == slots.astype(jnp.float32), gate[:, None, :], 0.0)
        weight = weight.reshape(experts * count, rows)
        high = weight.astype(jnp.bfloat16).astype(jnp.float32)
        out_ref[:rows, :] = high.T.astype(jnp.bfloat16)
        out_ref[rows:, :] = (weight - high).T.astype(jnp.bfloat16)
        first += count


def coefficients(ids_t, gates_t, experts, pieces):
    rows = ids_t.shape[1]
    width = experts * MOST // pieces
    return pl.pallas_call(
        coefficients_kernel,
        out_shape=[jax.ShapeDtypeStruct((2 * rows, width), jnp.bfloat16)] * pieces,
        compiler_params=pltpu.CompilerParams(vmem_limit_bytes=32 << 20),
        cost_estimate=pl.CostEstimate(
            flops=2 * experts * rows * rows,
            bytes_accessed=4 * rows * experts * MOST,
            transcendentals=0,
        ),
        name="coefficients",
    )(ids_t, gates_t)


def combine_kernel(weight_ref, values_ref, *refs):
    *start_refs, out_ref = refs
    rows = out_ref.shape[0]
    sums = jnp.dot(weight_ref[...], values_ref[...], preferred_element_type=jnp.float32)
    total = sums[:rows] + sums[rows:]
    if start_refs:
        total = start_refs[0][...] + total
    out_ref[...] = total.astype(out_ref.dtype)


def combine(weight, values, start, dtype):
    depth, width = values.shape
    rows = weight.shape[0] // 2
    part = 512
    column = pl.BlockSpec((rows, part), lambda i: (0, i))
    return pl.pallas_call(
        combine_kernel,
        out_shape=jax.ShapeDtypeStruct((rows, width), dtype),
        grid=(width // part,),
        in_specs=[
            pl.BlockSpec(weight.shape, lambda i: (0, 0)),
            pl.BlockSpec((depth, part), lambda i: (0, i)),
        ]
        + [column] * len(start),
        out_specs=column,
        compiler_params=pltpu.CompilerParams(vmem_limit_bytes=32 << 20),
        cost_estimate=pl.CostEstimate(
            flops=2 * weight.size * width,
            bytes_accessed=2 * (depth + rows) * width,
            transcendentals=0,
        ),
        name="combine",
    )(weight, values, *start)


def exchange(rows):
    return lax.all_to_all(rows, AXES, split_axis=0, concat_axis=0, tiled=True)


def body(tokens, expert_ids, route_gates, expert_weights):
    groups = lax.axis_size("expert")
    experts = expert_weights.shape[0] * groups
    model = tokens.shape[1]
    ids_t = expert_ids.T
    gates_t = route_gates.T
    half = MOST // 2
    out_a = dispatch(ids_t, tokens, experts, 0, half)
    out_b = dispatch(ids_t, tokens, experts, half, half)
    in_a = exchange(out_a)
    in_a, out_b, expert_weights = lax.optimization_barrier((in_a, out_b, expert_weights))
    weights = lax.all_to_all(expert_weights, "tensor", split_axis=0, concat_axis=0, tiled=True)
    in_a, out_b, weights = lax.optimization_barrier((in_a, out_b, weights))
    in_b = exchange(out_b)
    done_a = expert_ffn(in_a.reshape(experts * half, model), weights)
    done_a, in_b, ids_t, gates_t = lax.optimization_barrier((done_a, in_b, ids_t, gates_t))
    back_a = exchange(done_a.reshape(experts, half, model))
    done_b = expert_ffn(in_b.reshape(experts * half, model), weights)
    gates_a, gates_b = coefficients(ids_t, gates_t, experts, 2)
    done_b, back_a, gates_a, gates_b = lax.optimization_barrier(
        (done_b, back_a, gates_a, gates_b)
    )
    back_b = exchange(done_b.reshape(experts, half, model))
    part = combine(gates_a, back_a.reshape(experts * half, model), (), jnp.float32)
    return combine(gates_b, back_b.reshape(experts * half, model), (part,), jnp.bfloat16)


def solution(mesh):
    in_specs = (
        P(AXES, None),
        P(AXES, None),
        P(AXES, None),
        P("expert", None, "tensor", None),
    )
    return jax.shard_map(
        body, mesh=mesh, in_specs=in_specs, out_specs=P(AXES, None), check_vma=False
    )
```

time: 370 us -> 362 us (0.978)
  blocking collectives: 332 us -> 111 us
  waiting for transfers between devices: 0 us -> 170 us
  starting transfers between devices: 0 us -> 28.8 us
  Pallas kernels: 34.9 us -> 47.2 us
    all_to_all x2 -> x0, blocking collectives: 222 us -> none  [the longest x1 112 us: body(): lax.all_to_all(outputs.reshape(experts, MOST, model), AXES, split_axis=0,...]
    all_to_all x0 -> x4, waiting for transfers between devices: none -> 170 us  [exchange(): return lax.all_to_all(rows, AXES, split_axis=0, concat_axis=0, tiled=True)]
    all_to_all x0 -> x4, starting transfers between devices: none -> 28.8 us  [exchange(): return lax.all_to_all(rows, AXES, split_axis=0, concat_axis=0, tiled=True)]
    pallas_call x1 -> x3, Pallas kernels: 3.62 us -> 9.29 us  [the longest x2 8.66 us: dispatch(): pl.pallas_call(functools.partial(dispatch_kernel, first), out_shape=pltpu...]
    pallas_call x1 -> x2, Pallas kernels: 4.99 us -> 8.64 us  [combine(): pl.pallas_call(combine_kernel, out_shape=jax.ShapeDtypeStruct((rows, widt...]
    pallas_call x1 -> x2, Pallas kernels: 26.3 us -> 29.3 us  [expert_ffn(): pl.pallas_call(ffn_kernel, out_shape=jax.ShapeDtypeStruct((count, model),...]
  transfers between devices with their start and end apart: 0 -> 4, of which waited for: 0 -> 4; matrix products, arithmetic and copies ran while one was open for 0% -> 0% of each run, Pallas kernels for 0% -> 11%
where the time goes in v4:
time: 362 us
  waiting for transfers between devices  170 us (47%)
  blocking collectives  111 us (31%)
  Pallas kernels  47.2 us (13%)
  starting transfers between devices  28.8 us (8%)
  local copies, waits for them, and re-layouts  3.94 us (1%)
    all_to_all x4, waiting for transfers between devices, exchange(): return lax.all_to_all(rows, AXES, split_axis=0, concat_axis=0, tiled=True)  170 us
    all_to_all x1, blocking collectives, body(): lax.all_to_all(expert_weights, 'tensor', split_axis=0, concat_axis=0, til...  111 us
    pallas_call x2, Pallas kernels, expert_ffn(): pl.pallas_call(ffn_kernel, out_shape=jax.ShapeDtypeStruct((count, model),...  29.3 us
    all_to_all x4, starting transfers between devices, exchange(): return lax.all_to_all(rows, AXES, split_axis=0, concat_axis=0, tiled=True)  28.8 us
    pallas_call x2, Pallas kernels, dispatch(): pl.pallas_call(functools.partial(dispatch_kernel, first), out_shape=pltpu...  8.66 us
    pallas_call x2, Pallas kernels, combine(): pl.pallas_call(combine_kernel, out_shape=jax.ShapeDtypeStruct((rows, widt...  8.64 us
  transfers between devices with their start and end apart: 4, of which 4 were waited for; matrix products, arithmetic and copies ran while one was open for 0% of the time, Pallas kernels for 11%

profile of v4, /device:TPU:6, one launch (start us, length us, event | category | flops | bytes accessed | tf_op | source)
XLA Modules:
  0.0 361.5 jit_solution(4408078474861794068)
XLA Ops:
  0.0 4.3 %dispatch.2 = bf16[128,8,2048]{2,1,0:T(8,128)(2,1)} custom-call(s32[8,128]{1,0:T(8,128)} %bitcast.10, bf16[128,2048]{1,0:T(8,128)(2,1)} %tokens_hbm.3), custom_call_target="tpu_custom_call" | custom-call | flops 536870912 | bytes 4718592 | tf_op jit(solution)/shard_map/dispatch/pallas_call | solution.py:57
  4.4 10.9 %all-to-all-start = ((bf16[128,8,2048]{2,1,0:T(8,128)(2,1)}), bf16[128,8,2048]{2,1,0:T(8,128)(2,1)}, u32[]{:S(2)}, u32[]{:S(2)}) async-start(bf16[128,8,2048]{2,1,0:T(8,128)(2,1)} %dispatch.2), calls=%async_computation | async-start | bytes 8388608 | tf_op jit(solution)/shard_map/all_to_all | solution.py:191
  15.3 4.3 %dispatch.3 = bf16[128,8,2048]{2,1,0:T(8,128)(2,1)} custom-call(s32[8,128]{1,0:T(8,128)} %bitcast.11, bf16[128,2048]{1,0:T(8,128)(2,1)} %tokens_hbm.3), custom_call_target="tpu_custom_call" | custom-call | flops 536870912 | bytes 4718592 | tf_op jit(solution)/shard_map/dispatch/pallas_call | solution.py:57
  19.6 48.7 %all-to-all-done = bf16[128,8,2048]{2,1,0:T(8,128)(2,1)} async-done(((bf16[128,8,2048]{2,1,0:T(8,128)(2,1)}), bf16[128,8,2048]{2,1,0:T(8,128)(2,1)}, u32[]{:S(2)}, u32[]{:S(2)}) %all-to-all-start) | async-done | bytes 4194336 | tf_op jit(solution)/shard_map/all_to_all | solution.py:191
  68.4 111.2 %all_to_all.25.weights_ref = bf16[16,3,48,2048]{3,2,1,0:T(8,128)(2,1)} all-to-all(bf16[16,3,48,2048]{3,2,1,0:T(8,128)(2,1)} %param.7), channel_id=1, replica_groups=mesh['expert'=8,'tensor'=16] {'tensor'}, dimensions={0} | all-to-all | bytes 18874368 | tf_op jit(solution)/shard_map/all_to_all | solution.py:205
  179.6 8.1 %all-to-all-start.2 = ((bf16[128,8,2048]{2,1,0:T(8,128)(2,1)}), bf16[128,8,2048]{2,1,0:T(8,128)(2,1)}, u32[]{:S(2)}, u32[]{:S(2)}) async-start(bf16[128,8,2048]{2,1,0:T(8,128)(2,1)} %dispatch.3), calls=%async_computation.2 | async-start | bytes 8388608 | tf_op jit(solution)/shard_map/all_to_all | solution.py:191
  187.7 14.7 %expert_ffn.2 = bf16[1024,2048]{1,0:T(8,128)(2,1)S(1)} custom-call(bf16[1024,2048]{1,0:T(8,128)(2,1)} %bitcast.1.rows_ref, bf16[16,3,48,2048]{3,2,1,0:T(8,128)(2,1)} %all_to_all.25.weights_ref), custom_call_target="tpu_custom_call" | custom-call | flops 9663676416 | bytes 17825792 | tf_op jit(solution)/shard_map/expert_ffn/pallas_call | solution.py:99
  202.3 0.0 copy-start
  202.3 2.0 copy-done
  204.3 36.4 %all-to-all-done.2 = bf16[128,8,2048]{2,1,0:T(8,128)(2,1)} async-done(((bf16[128,8,2048]{2,1,0:T(8,128)(2,1)}), bf16[128,8,2048]{2,1,0:T(8,128)(2,1)}, u32[]{:S(2)}, u32[]{:S(2)}) %all-to-all-start.2) | async-done | bytes 4194336 | tf_op jit(solution)/shard_map/all_to_all | solution.py:191
  240.7 0.0 copy-start.2
  240.7 0.0 copy-start.3
  240.7 4.9 %all-to-all-start.3 = ((bf16[128,8,2048]{2,1,0:T(8,128)(2,1)}), bf16[128,8,2048]{2,1,0:T(8,128)(2,1)}, u32[]{:S(2)}, u32[]{:S(2)}) async-start(bf16[128,8,2048]{2,1,0:T(8,128)(2,1)} %bitcast.8), calls=%async_computation.3 | async-start | bytes 8388608 | tf_op jit(solution)/shard_map/all_to_all | solution.py:191
  245.7 0.0 copy-done.2
  245.7 0.0 copy-done.3
  245.7 0.6 coefficients.1
  246.3 14.7 %expert_ffn.3 = bf16[1024,2048]{1,0:T(8,128)(2,1)S(1)} custom-call(bf16[1024,2048]{1,0:T(8,128)(2,1)} %bitcast.3.rows_ref, bf16[16,3,48,2048]{3,2,1,0:T(8,128)(2,1)} %all_to_all.25.weights_ref), custom_call_target="tpu_custom_call" | custom-call | flops 9663676416 | bytes 17825792 | tf_op jit(solution)/shard_map/expert_ffn/pallas_call | solution.py:99
  261.0 0.0 copy-start.1
  261.0 1.9 copy-done.1
  262.9 35.9 %all-to-all-done.3 = bf16[128,8,2048]{2,1,0:T(8,128)(2,1)} async-done(((bf16[128,8,2048]{2,1,0:T(8,128)(2,1)}), bf16[128,8,2048]{2,1,0:T(8,128)(2,1)}, u32[]{:S(2)}, u32[]{:S(2)}) %all-to-all-start.3) | async-done | bytes 4194336 | tf_op jit(solution)/shard_map/all_to_all | solution.py:191
  298.8 4.9 %all-to-all-start.4 = ((bf16[128,8,2048]{2,1,0:T(8,128)(2,1)}), bf16[128,8,2048]{2,1,0:T(8,128)(2,1)}, u32[]{:S(2)}, u32[]{:S(2)}) async-start(bf16[128,8,2048]{2,1,0:T(8,128)(2,1)} %bitcast.9), calls=%async_computation.4 | async-start | bytes 8388608 | tf_op jit(solution)/shard_map/all_to_all | solution.py:191
  303.7 3.9 %combine.2.refs_0_ = f32[128,2048]{1,0:T(8,128)S(1)} custom-call(bf16[256,1024]{1,0:T(8,128)(2,1)S(1)} %get-tuple-element.35.weight_ref, bf16[1024,2048]{1,0:T(8,128)(2,1)} %bitcast.7.values_ref), custom_call_target="tpu_custom_call" | custom-call | flops 1073741824 | bytes 4718592 | tf_op jit(solution)/shard_map/combine/pallas_call | solution.py:170
  307.7 49.1 %all-to-all-done.4 = bf16[128,8,2048]{2,1,0:T(8,128)(2,1)} async-done(((bf16[128,8,2048]{2,1,0:T(8,128)(2,1)}), bf16[128,8,2048]{2,1,0:T(8,128)(2,1)}, u32[]{:S(2)}, u32[]{:S(2)}) %all-to-all-start.4) | async-done | bytes 4194336 | tf_op jit(solution)/shard_map/all_to_all | solution.py:191
  356.8 4.7 %combine.3 = bf16[128,2048]{1,0:T(8,128)(2,1)} custom-call(bf16[256,1024]{1,0:T(8,128)(2,1)S(1)} %get-tuple-element.33.weight_ref, bf16[1024,2048]{1,0:T(8,128)(2,1)} %bitcast.6.values_ref, f32[128,2048]{1,0:T(8,128)S(1)} %combine.2.refs_0_), custom_call_target="tpu_custom_call" | custom-call | flops 1073741824 | bytes 4718592 | tf_op jit(solution)/shard_map/combine/pallas_call | solution.py:170
Async XLA Ops:
  4.4 64.0 %all-to-all-start = ((bf16[128,8,2048]{2,1,0:T(8,128)(2,1)}), bf16[128,8,2048]{2,1,0:T(8,128)(2,1)}, u32[]{:S(2)}, u32[]{:S(2)}) async-start(bf16[128,8,2048]{2,1,0:T(8,128)(2,1)} %dispatch.2), calls=%async_computation | async-start | bytes 8388608 | tf_op jit(solution)/shard_map/all_to_all | solution.py:191
  179.6 61.1 %all-to-all-start.2 = ((bf16[128,8,2048]{2,1,0:T(8,128)(2,1)}), bf16[128,8,2048]{2,1,0:T(8,128)(2,1)}, u32[]{:S(2)}, u32[]{:S(2)}) async-start(bf16[128,8,2048]{2,1,0:T(8,128)(2,1)} %dispatch.3), calls=%async_computation.2 | async-start | bytes 8388608 | tf_op jit(solution)/shard_map/all_to_all | solution.py:191
  202.3 2.0 copy-start
  240.7 4.9 %copy-start.2 = (s32[128,8]{0,1:T(8,128)S(1)}, s32[128,8]{0,1:T(8,128)}, u32[]{:S(2)}) copy-start(s32[128,8]{0,1:T(8,128)} %param.5) | copy-start | bytes 12292
  240.7 5.0 %copy-start.3 = (f32[128,8]{0,1:T(8,128)S(1)}, f32[128,8]{0,1:T(8,128)}, u32[]{:S(2)}) copy-start(f32[128,8]{0,1:T(8,128)} %param.6) | copy-start | bytes 12292
  240.7 58.1 %all-to-all-start.3 = ((bf16[128,8,2048]{2,1,0:T(8,128)(2,1)}), bf16[128,8,2048]{2,1,0:T(8,128)(2,1)}, u32[]{:S(2)}, u32[]{:S(2)}) async-start(bf16[128,8,2048]{2,1,0:T(8,128)(2,1)} %bitcast.8), calls=%async_computation.3 | async-start | bytes 8388608 | tf_op jit(solution)/shard_map/all_to_all | solution.py:191
  261.0 2.0 copy-start.1
  298.8 58.0 %all-to-all-start.4 = ((bf16[128,8,2048]{2,1,0:T(8,128)(2,1)}), bf16[128,8,2048]{2,1,0:T(8,128)(2,1)}, u32[]{:S(2)}, u32[]{:S(2)}) async-start(bf16[128,8,2048]{2,1,0:T(8,128)(2,1)} %bitcast.9), calls=%async_computation.4 | async-start | bytes 8388608 | tf_op jit(solution)/shard_map/all_to_all | solution.py:191

commit v5 on v4

--- a/solution.py
+++ b/solution.py
@@ -53,7 +53,7 @@
 
 def dispatch(ids_t, tokens, experts, first, count):
     rows, width = tokens.shape
-    part = 32
+    part = 64
     return pl.pallas_call(
         functools.partial(dispatch_kernel, first),
         out_shape=pltpu.HBM((experts, count, width), jnp.bfloat16),
@@ -165,7 +165,7 @@
 def combine(weight, values, start, dtype):
     depth, width = values.shape
     rows = weight.shape[0] // 2
-    part = 512
+    part = 1024
     column = pl.BlockSpec((rows, part), lambda i: (0, i))
     return pl.pallas_call(
         combine_kernel,

time: 362 us -> 361 us (level)
  transfers between devices with their start and end apart: 4 -> 4, of which waited for: 4 -> 4; matrix products, arithmetic and copies ran while one was open for 0% -> 0% of each run, Pallas kernels for 11% -> 10%
where the time goes in v5:
time: 361 us; the launch traced here: 360 us
  waiting for transfers between devices  172 us (48%)
  blocking collectives  111 us (31%)
  Pallas kernels  44.3 us (12%)
  starting transfers between devices  28.8 us (8%)
  local copies, waits for them, and re-layouts  3.94 us (1%)
    all_to_all x4, waiting for transfers between devices, exchange(): return lax.all_to_all(rows, AXES, split_axis=0, concat_axis=0, tiled=True)  172 us
    all_to_all x1, blocking collectives, body(): lax.all_to_all(expert_weights, 'tensor', split_axis=0, concat_axis=0, til...  111 us
    pallas_call x2, Pallas kernels, expert_ffn(): pl.pallas_call(ffn_kernel, out_shape=jax.ShapeDtypeStruct((count, model),...  29.3 us
    all_to_all x4, starting transfers between devices, exchange(): return lax.all_to_all(rows, AXES, split_axis=0, concat_axis=0, tiled=True)  28.8 us
    pallas_call x2, Pallas kernels, dispatch(): pl.pallas_call(functools.partial(dispatch_kernel, first), out_shape=pltpu...  7.57 us
  transfers between devices with their start and end apart: 4, of which 4 were waited for; matrix products, arithmetic and copies ran while one was open for 0% of the time, Pallas kernels for 10%

profile of v5, /device:TPU:6, one launch (start us, length us, event | category | flops | bytes accessed | tf_op | source)
XLA Modules:
  0.0 360.0 jit_solution(14059981881663046849)
XLA Ops:
  0.0 3.8 %dispatch.2 = bf16[128,8,2048]{2,1,0:T(8,128)(2,1)} custom-call(s32[8,128]{1,0:T(8,128)} %bitcast.10, bf16[128,2048]{1,0:T(8,128)(2,1)} %tokens_hbm.3), custom_call_target="tpu_custom_call" | custom-call | flops 536870912 | bytes 4718592 | tf_op jit(solution)/shard_map/dispatch/pallas_call | solution.py:57
  3.8 10.9 %all-to-all-start = ((bf16[128,8,2048]{2,1,0:T(8,128)(2,1)}), bf16[128,8,2048]{2,1,0:T(8,128)(2,1)}, u32[]{:S(2)}, u32[]{:S(2)}) async-start(bf16[128,8,2048]{2,1,0:T(8,128)(2,1)} %dispatch.2), calls=%async_computation | async-start | bytes 8388608 | tf_op jit(solution)/shard_map/all_to_all | solution.py:191
  14.7 3.8 %dispatch.3 = bf16[128,8,2048]{2,1,0:T(8,128)(2,1)} custom-call(s32[8,128]{1,0:T(8,128)} %bitcast.11, bf16[128,2048]{1,0:T(8,128)(2,1)} %tokens_hbm.3), custom_call_target="tpu_custom_call" | custom-call | flops 536870912 | bytes 4718592 | tf_op jit(solution)/shard_map/dispatch/pallas_call | solution.py:57
  18.5 49.3 %all-to-all-done = bf16[128,8,2048]{2,1,0:T(8,128)(2,1)} async-done(((bf16[128,8,2048]{2,1,0:T(8,128)(2,1)}), bf16[128,8,2048]{2,1,0:T(8,128)(2,1)}, u32[]{:S(2)}, u32[]{:S(2)}) %all-to-all-start) | async-done | bytes 4194336 | tf_op jit(solution)/shard_map/all_to_all | solution.py:191
  67.8 111.2 %all_to_all.25.weights_ref = bf16[16,3,48,2048]{3,2,1,0:T(8,128)(2,1)} all-to-all(bf16[16,3,48,2048]{3,2,1,0:T(8,128)(2,1)} %param.7), channel_id=1, replica_groups=mesh['expert'=8,'tensor'=16] {'tensor'}, dimensions={0} | all-to-all | bytes 18874368 | tf_op jit(solution)/shard_map/all_to_all | solution.py:205
  179.0 8.1 %all-to-all-start.2 = ((bf16[128,8,2048]{2,1,0:T(8,128)(2,1)}), bf16[128,8,2048]{2,1,0:T(8,128)(2,1)}, u32[]{:S(2)}, u32[]{:S(2)}) async-start(bf16[128,8,2048]{2,1,0:T(8,128)(2,1)} %dispatch.3), calls=%async_computation.2 | async-start | bytes 8388608 | tf_op jit(solution)/shard_map/all_to_all | solution.py:191
  187.1 14.6 %expert_ffn.2 = bf16[1024,2048]{1,0:T(8,128)(2,1)S(1)} custom-call(bf16[1024,2048]{1,0:T(8,128)(2,1)} %bitcast.1.rows_ref, bf16[16,3,48,2048]{3,2,1,0:T(8,128)(2,1)} %all_to_all.25.weights_ref), custom_call_target="tpu_custom_call" | custom-call | flops 9663676416 | bytes 17825792 | tf_op jit(solution)/shard_map/expert_ffn/pallas_call | solution.py:99
  201.7 0.0 copy-start
  201.8 2.0 copy-done
  203.7 36.4 %all-to-all-done.2 = bf16[128,8,2048]{2,1,0:T(8,128)(2,1)} async-done(((bf16[128,8,2048]{2,1,0:T(8,128)(2,1)}), bf16[128,8,2048]{2,1,0:T(8,128)(2,1)}, u32[]{:S(2)}, u32[]{:S(2)}) %all-to-all-start.2) | async-done | bytes 4194336 | tf_op jit(solution)/shard_map/all_to_all | solution.py:191
  240.2 0.0 copy-start.2
  240.2 0.0 copy-start.3
  240.2 4.9 %all-to-all-start.3 = ((bf16[128,8,2048]{2,1,0:T(8,128)(2,1)}), bf16[128,8,2048]{2,1,0:T(8,128)(2,1)}, u32[]{:S(2)}, u32[]{:S(2)}) async-start(bf16[128,8,2048]{2,1,0:T(8,128)(2,1)} %bitcast.8), calls=%async_computation.3 | async-start | bytes 8388608 | tf_op jit(solution)/shard_map/all_to_all | solution.py:191
  245.1 0.0 copy-done.2
  245.1 0.0 copy-done.3
  245.1 0.6 coefficients.1
  245.8 14.7 %expert_ffn.3 = bf16[1024,2048]{1,0:T(8,128)(2,1)S(1)} custom-call(bf16[1024,2048]{1,0:T(8,128)(2,1)} %bitcast.3.rows_ref, bf16[16,3,48,2048]{3,2,1,0:T(8,128)(2,1)} %all_to_all.25.weights_ref), custom_call_target="tpu_custom_call" | custom-call | flops 9663676416 | bytes 17825792 | tf_op jit(solution)/shard_map/expert_ffn/pallas_call | solution.py:99
  260.4 0.0 copy-start.1
  260.4 1.9 copy-done.1
  262.4 35.9 %all-to-all-done.3 = bf16[128,8,2048]{2,1,0:T(8,128)(2,1)} async-done(((bf16[128,8,2048]{2,1,0:T(8,128)(2,1)}), bf16[128,8,2048]{2,1,0:T(8,128)(2,1)}, u32[]{:S(2)}, u32[]{:S(2)}) %all-to-all-start.3) | async-done | bytes 4194336 | tf_op jit(solution)/shard_map/all_to_all | solution.py:191
  298.3 4.9 %all-to-all-start.4 = ((bf16[128,8,2048]{2,1,0:T(8,128)(2,1)}), bf16[128,8,2048]{2,1,0:T(8,128)(2,1)}, u32[]{:S(2)}, u32[]{:S(2)}) async-start(bf16[128,8,2048]{2,1,0:T(8,128)(2,1)} %bitcast.9), calls=%async_computation.4 | async-start | bytes 8388608 | tf_op jit(solution)/shard_map/all_to_all | solution.py:191
  303.2 3.1 combine.2.refs_0_
  306.3 50.0 %all-to-all-done.4 = bf16[128,8,2048]{2,1,0:T(8,128)(2,1)} async-done(((bf16[128,8,2048]{2,1,0:T(8,128)(2,1)}), bf16[128,8,2048]{2,1,0:T(8,128)(2,1)}, u32[]{:S(2)}, u32[]{:S(2)}) %all-to-all-start.4) | async-done | bytes 4194336 | tf_op jit(solution)/shard_map/all_to_all | solution.py:191
  356.3 3.7 %combine.3 = bf16[128,2048]{1,0:T(8,128)(2,1)} custom-call(bf16[256,1024]{1,0:T(8,128)(2,1)S(1)} %get-tuple-element.33.weight_ref, bf16[1024,2048]{1,0:T(8,128)(2,1)} %bitcast.6.values_ref, f32[128,2048]{1,0:T(8,128)S(1)} %combine.2.refs_0_), custom_call_target="tpu_custom_call" | custom-call | flops 1073741824 | bytes 4718592 | tf_op jit(solution)/shard_map/combine/pallas_call | solution.py:170
Async XLA Ops:
  3.8 64.0 %all-to-all-start = ((bf16[128,8,2048]{2,1,0:T(8,128)(2,1)}), bf16[128,8,2048]{2,1,0:T(8,128)(2,1)}, u32[]{:S(2)}, u32[]{:S(2)}) async-start(bf16[128,8,2048]{2,1,0:T(8,128)(2,1)} %dispatch.2), calls=%async_computation | async-start | bytes 8388608 | tf_op jit(solution)/shard_map/all_to_all | solution.py:191
  179.0 61.1 %all-to-all-start.2 = ((bf16[128,8,2048]{2,1,0:T(8,128)(2,1)}), bf16[128,8,2048]{2,1,0:T(8,128)(2,1)}, u32[]{:S(2)}, u32[]{:S(2)}) async-start(bf16[128,8,2048]{2,1,0:T(8,128)(2,1)} %dispatch.3), calls=%async_computation.2 | async-start | bytes 8388608 | tf_op jit(solution)/shard_map/all_to_all | solution.py:191
  201.7 2.0 copy-start
  240.2 4.9 %copy-start.2 = (s32[128,8]{0,1:T(8,128)S(1)}, s32[128,8]{0,1:T(8,128)}, u32[]{:S(2)}) copy-start(s32[128,8]{0,1:T(8,128)} %param.5) | copy-start | bytes 12292
  240.2 5.0 %copy-start.3 = (f32[128,8]{0,1:T(8,128)S(1)}, f32[128,8]{0,1:T(8,128)}, u32[]{:S(2)}) copy-start(f32[128,8]{0,1:T(8,128)} %param.6) | copy-start | bytes 12292
  240.2 58.1 %all-to-all-start.3 = ((bf16[128,8,2048]{2,1,0:T(8,128)(2,1)}), bf16[128,8,2048]{2,1,0:T(8,128)(2,1)}, u32[]{:S(2)}, u32[]{:S(2)}) async-start(bf16[128,8,2048]{2,1,0:T(8,128)(2,1)} %bitcast.8), calls=%async_computation.3 | async-start | bytes 8388608 | tf_op jit(solution)/shard_map/all_to_all | solution.py:191
  260.4 2.0 copy-start.1
  298.3 58.0 %all-to-all-start.4 = ((bf16[128,8,2048]{2,1,0:T(8,128)(2,1)}), bf16[128,8,2048]{2,1,0:T(8,128)(2,1)}, u32[]{:S(2)}, u32[]{:S(2)}) async-start(bf16[128,8,2048]{2,1,0:T(8,128)(2,1)} %bitcast.9), calls=%async_computation.4 | async-start | bytes 8388608 | tf_op jit(solution)/shard_map/all_to_all | solution.py:191

commit v6 on v5

--- a/solution.py
+++ b/solution.py
@@ -56,7 +56,7 @@
     part = 64
     return pl.pallas_call(
         functools.partial(dispatch_kernel, first),
-        out_shape=pltpu.HBM((experts, count, width), jnp.bfloat16),
+        out_shape=jax.ShapeDtypeStruct((experts, count, width), jnp.bfloat16),
         grid=(experts // part,),
         in_specs=[pl.BlockSpec(memory_space=pltpu.HBM)] * 2,
         out_specs=pl.BlockSpec((part, count, width), lambda i: (i, 0, 0)),
@@ -79,40 +79,51 @@
     )
 
 
-def ffn_kernel(rows_ref, weights_ref, out_ref):
+def ffn_kernel(first, rows_ref, weights_ref, out_hbm, held, sem):
     blocks, _, width_block, model = weights_ref.shape
     hidden_units = blocks * width_block
+    _, part, count, _ = held.shape
     contract_last = (((1,), (1,)), ((), ()))
-    x = rows_ref[...]
     w_gate = weights_ref[:, 0].reshape(hidden_units, model)
     w_up = weights_ref[:, 1].reshape(hidden_units, model)
     w_down = weights_ref[:, 2].reshape(hidden_units, model)
-    gate = lax.dot_general(x, w_gate, contract_last, preferred_element_type=jnp.float32)
-    up = lax.dot_general(x, w_up, contract_last, preferred_element_type=jnp.float32)
-    hidden = (gate / (1.0 + jnp.exp(-gate)) * up).astype(jnp.bfloat16)
-    out_ref[...] = jnp.dot(hidden, w_down, preferred_element_type=jnp.float32).astype(jnp.bfloat16)
-
-
-def expert_ffn(rows, weights):
-    count, model = rows.shape
-    part = 256
-    return pl.pallas_call(
-        ffn_kernel,
-        out_shape=jax.ShapeDtypeStruct((count, model), jnp.bfloat16),
-        grid=(count // part,),
-        in_specs=[
-            pl.BlockSpec((part, model), lambda i: (i, 0)),
-            pl.BlockSpec(weights.shape, lambda i: (0, 0, 0, 0), pipeline_mode=pl.Buffered(1)),
+    writes = []
+    for tile in range(rows_ref.shape[0] // part):
+        here = pl.ds(tile * part, part)
+        x = rows_ref[here, first : first + count, :].reshape(part * count, model)
+        gate = lax.dot_general(x, w_gate, contract_last, preferred_element_type=jnp.float32)
+        up = lax.dot_general(x, w_up, contract_last, preferred_element_type=jnp.float32)
+        hidden = (gate / (1.0 + jnp.exp(-gate)) * up).astype(jnp.bfloat16)
+        out = jnp.dot(hidden, w_down, preferred_element_type=jnp.float32).astype(jnp.bfloat16)
+        held[tile] = out.reshape(part, count, model)
+        writes.append(pltpu.make_async_copy(held.at[tile], out_hbm.at[here], sem.at[tile]))
+        writes[-1].start()
+    for write in writes:
+        write.wait()
+
+
+def expert_ffn(arrived, weights, first, count):
+    sources, _, model = arrived.shape
+    part = 256 // count
+    tiles = sources // part
+    rows = sources * count
+    return pl.pallas_call(
+        functools.partial(ffn_kernel, first),
+        out_shape=pltpu.HBM((sources, count, model), jnp.bfloat16),
+        in_specs=[pl.BlockSpec(memory_space=pltpu.VMEM)] * 2,
+        out_specs=pl.BlockSpec(memory_space=pltpu.HBM),
+        scratch_shapes=[
+            pltpu.VMEM((tiles, part, count, model), jnp.bfloat16),
+            pltpu.SemaphoreType.DMA((tiles,)),
         ],
-        out_specs=pl.BlockSpec((part, model), lambda i: (i, 0)),
-        compiler_params=pltpu.CompilerParams(vmem_limit_bytes=48 << 20),
-        cost_estimate=pl.CostEstimate(
-            flops=2 * count * weights.size,
-            bytes_accessed=2 * (2 * rows.size + weights.size),
-            transcendentals=count * weights.size // (3 * model),
+        compiler_params=pltpu.CompilerParams(vmem_limit_bytes=32 << 20),
+        cost_estimate=pl.CostEstimate(
+            flops=2 * rows * weights.size,
+            bytes_accessed=2 * (2 * rows * model + weights.size),
+            transcendentals=rows * weights.size // (3 * model),
         ),
         name="expert_ffn",
-    )(rows, weights)
+    )(arrived, weights)
 
 
 def coefficients_kernel(ids_ref, gates_ref, *out_refs):
@@ -198,22 +209,20 @@
     ids_t = expert_ids.T
     gates_t = route_gates.T
     half = MOST // 2
-    out_a = dispatch(ids_t, tokens, experts, 0, half)
-    out_b = dispatch(ids_t, tokens, experts, half, half)
-    in_a = exchange(out_a)
-    in_a, out_b, expert_weights = lax.optimization_barrier((in_a, out_b, expert_weights))
+    outgoing = dispatch(ids_t, tokens, experts, 0, MOST)
+    outgoing, expert_weights = lax.optimization_barrier((outgoing, expert_weights))
     weights = lax.all_to_all(expert_weights, "tensor", split_axis=0, concat_axis=0, tiled=True)
-    in_a, out_b, weights = lax.optimization_barrier((in_a, out_b, weights))
-    in_b = exchange(out_b)
-    done_a = expert_ffn(in_a.reshape(experts * half, model), weights)
-    done_a, in_b, ids_t, gates_t = lax.optimization_barrier((done_a, in_b, ids_t, gates_t))
-    back_a = exchange(done_a.reshape(experts, half, model))
-    done_b = expert_ffn(in_b.reshape(experts * half, model), weights)
+    outgoing, weights = lax.optimization_barrier((outgoing, weights))
+    arrived = exchange(outgoing)
+    done_a = expert_ffn(arrived, weights, 0, half)
+    done_a, ids_t, gates_t = lax.optimization_barrier((done_a, ids_t, gates_t))
+    back_a = exchange(done_a)
+    done_b = expert_ffn(arrived, weights, half, half)
     gates_a, gates_b = coefficients(ids_t, gates_t, experts, 2)
     done_b, back_a, gates_a, gates_b = lax.optimization_barrier(
         (done_b, back_a, gates_a, gates_b)
     )
-    back_b = exchange(done_b.reshape(experts, half, model))
+    back_b = exchange(done_b)
     part = combine(gates_a, back_a.reshape(experts * half, model), (), jnp.float32)
     return combine(gates_b, back_b.reshape(experts * half, model), (part,), jnp.bfloat16)
 

time: 361 us -> 358 us (level)
  blocking collectives: 111 us -> 222 us
  waiting for transfers between devices: 172 us -> 84.3 us
  starting transfers between devices: 28.8 us -> 10.4 us
  Pallas kernels: 44.3 us -> 33.1 us
    all_to_all x0 -> x1, blocking collectives: none -> 106 us  [exchange(): return lax.all_to_all(rows, AXES, split_axis=0, concat_axis=0, tiled=True)]
    all_to_all x4 -> x2, waiting for transfers between devices: 172 us -> 84.3 us  [exchange(): return lax.all_to_all(rows, AXES, split_axis=0, concat_axis=0, tiled=True)]
    all_to_all x4 -> x2, starting transfers between devices: 28.8 us -> 10.4 us  [exchange(): return lax.all_to_all(rows, AXES, split_axis=0, concat_axis=0, tiled=True)]
    pallas_call x4 -> x3, Pallas kernels: 36.9 us -> 25.6 us  [the longest x2 22.1 us: expert_ffn(): pl.pallas_call(functools.partial(ffn_kernel, first), out_shape=pltpu.HBM(...]
    all_to_all x1, blocking collectives: 111 us -> 116 us  [body(): lax.all_to_all(expert_weights, 'tensor', split_axis=0, concat_axis=0, til...]
  transfers between devices with their start and end apart: 4 -> 2, of which waited for: 4 -> 2; matrix products, arithmetic and copies ran while one was open for 0% -> 0% of each run, Pallas kernels for 10% -> 4%
where the time goes in v6:
time: 358 us; the launch traced here: 357 us
  blocking collectives  222 us (62%)
  waiting for transfers between devices  84.3 us (24%)
  Pallas kernels  33.1 us (9%)
  starting transfers between devices  10.4 us (3%)
  local copies, waits for them, and re-layouts  7.07 us (2%)
    all_to_all x1, blocking collectives, body(): lax.all_to_all(expert_weights, 'tensor', split_axis=0, concat_axis=0, til...  116 us
    all_to_all x1, blocking collectives, exchange(): return lax.all_to_all(rows, AXES, split_axis=0, concat_axis=0, tiled=True)  106 us
    all_to_all x2, waiting for transfers between devices, exchange(): return lax.all_to_all(rows, AXES, split_axis=0, concat_axis=0, tiled=True)  84.3 us
    pallas_call x2, Pallas kernels, expert_ffn(): pl.pallas_call(functools.partial(ffn_kernel, first), out_shape=pltpu.HBM(...  22.1 us
    all_to_all x2, starting transfers between devices, exchange(): return lax.all_to_all(rows, AXES, split_axis=0, concat_axis=0, tiled=True)  10.4 us
  transfers between devices with their start and end apart: 2, of which 2 were waited for; matrix products, arithmetic and copies ran while one was open for 0% of the time, Pallas kernels for 4%

profile of v6, /device:TPU:6, one launch (start us, length us, event | category | flops | bytes accessed | tf_op | source)
XLA Modules:
  0.0 357.2 jit_solution(10850044096804351933)
XLA Ops:
  0.0 3.6 dispatch.1
  3.6 115.8 %all_to_all.20.weights_ref = bf16[16,3,48,2048]{3,2,1,0:T(8,128)(2,1)S(1)} all-to-all(bf16[16,3,48,2048]{3,2,1,0:T(8,128)(2,1)} %param.7), channel_id=1, replica_groups=mesh['expert'=8,'tensor'=16] {'tensor'}, dimensions={0} | all-to-all | bytes 18874368 | tf_op jit(solution)/shard_map/all_to_all | solution.py:214
  119.4 0.0 copy-start
  119.4 106.4 %all_to_all.21.rows_ref = bf16[128,16,2048]{2,1,0:T(8,128)(2,1)S(1)} all-to-all(bf16[128,16,2048]{2,1,0:T(8,128)(2,1)S(1)} %dispatch.1), channel_id=1, replica_groups=mesh['expert'=8,'tensor'=16] {'expert','tensor'}, dimensions={0} | all-to-all | bytes 16777216 | tf_op jit(solution)/shard_map/all_to_all | solution.py:202
  225.8 0.0 copy-start.2
  225.8 11.1 %expert_ffn.3 = bf16[128,8,2048]{2,1,0:T(8,128)(2,1)} custom-call(bf16[128,16,2048]{2,1,0:T(8,128)(2,1)S(1)} %all_to_all.21.rows_ref, bf16[16,3,48,2048]{3,2,1,0:T(8,128)(2,1)S(1)} %all_to_all.20.weights_ref), custom_call_target="tpu_custom_call" | custom-call | flops 9663676416 | bytes 17825792 | tf_op jit(solution)/shard_map/expert_ffn/pallas_call | solution.py:110
  236.9 0.0 copy-done
  236.9 0.0 copy-done.2
  236.9 0.0 copy-start.4
  236.9 0.0 copy-start.5
  236.9 5.5 %all-to-all-start.2 = ((bf16[128,8,2048]{2,1,0:T(8,128)(2,1)}), bf16[128,8,2048]{2,1,0:T(8,128)(2,1)}, u32[]{:S(2)}, u32[]{:S(2)}) async-start(bf16[128,8,2048]{2,1,0:T(8,128)(2,1)} %expert_ffn.3), calls=%async_computation.2 | async-start | bytes 8388608 | tf_op jit(solution)/shard_map/all_to_all | solution.py:202
  242.4 0.0 copy-done.4
  242.5 0.0 copy-done.5
  242.5 0.6 coefficients.1
  243.1 0.0 copy-start.1
  243.1 3.7 %copy-done.1 = bf16[16,3,48,2048]{3,2,1,0:T(8,128)(2,1)S(1)} copy-done((bf16[16,3,48,2048]{3,2,1,0:T(8,128)(2,1)S(1)}, bf16[16,3,48,2048]{3,2,1,0:T(8,128)(2,1)}, u32[]{:S(2)}) %copy-start.1) | copy-done | bytes 9437208
  246.8 0.0 copy-start.3
  246.8 3.4 copy-done.3
  250.2 11.0 %expert_ffn.2 = bf16[128,8,2048]{2,1,0:T(8,128)(2,1)} custom-call(bf16[128,16,2048]{2,1,0:T(8,128)(2,1)S(1)} %copy-done.3, bf16[16,3,48,2048]{3,2,1,0:T(8,128)(2,1)S(1)} %copy-done.1), custom_call_target="tpu_custom_call" | custom-call | flops 9663676416 | bytes 17825792 | tf_op jit(solution)/shard_map/expert_ffn/pallas_call | solution.py:110
  261.2 34.3 %all-to-all-done.2 = bf16[128,8,2048]{2,1,0:T(8,128)(2,1)} async-done(((bf16[128,8,2048]{2,1,0:T(8,128)(2,1)}), bf16[128,8,2048]{2,1,0:T(8,128)(2,1)}, u32[]{:S(2)}, u32[]{:S(2)}) %all-to-all-start.2) | async-done | bytes 4194336 | tf_op jit(solution)/shard_map/all_to_all | solution.py:202
  295.5 4.9 %all-to-all-start.3 = ((bf16[128,8,2048]{2,1,0:T(8,128)(2,1)}), bf16[128,8,2048]{2,1,0:T(8,128)(2,1)}, u32[]{:S(2)}, u32[]{:S(2)}) async-start(bf16[128,8,2048]{2,1,0:T(8,128)(2,1)} %expert_ffn.2), calls=%async_computation.3 | async-start | bytes 8388608 | tf_op jit(solution)/shard_map/all_to_all | solution.py:202
  300.4 3.1 combine.2.refs_0_
  303.5 50.0 %all-to-all-done.3 = bf16[128,8,2048]{2,1,0:T(8,128)(2,1)} async-done(((bf16[128,8,2048]{2,1,0:T(8,128)(2,1)}), bf16[128,8,2048]{2,1,0:T(8,128)(2,1)}, u32[]{:S(2)}, u32[]{:S(2)}) %all-to-all-start.3) | async-done | bytes 4194336 | tf_op jit(solution)/shard_map/all_to_all | solution.py:202
  353.5 3.7 %combine.3 = bf16[128,2048]{1,0:T(8,128)(2,1)} custom-call(bf16[256,1024]{1,0:T(8,128)(2,1)S(1)} %get-tuple-element.27.weight_ref, bf16[1024,2048]{1,0:T(8,128)(2,1)} %bitcast.2.values_ref, f32[128,2048]{1,0:T(8,128)S(1)} %combine.2.refs_0_), custom_call_target="tpu_custom_call" | custom-call | flops 1073741824 | bytes 4718592 | tf_op jit(solution)/shard_map/combine/pallas_call | solution.py:181
Async XLA Ops:
  119.4 117.5 %copy-start = (bf16[16,3,48,2048]{3,2,1,0:T(8,128)(2,1)}, bf16[16,3,48,2048]{3,2,1,0:T(8,128)(2,1)S(1)}, u32[]{:S(2)}) copy-start(bf16[16,3,48,2048]{3,2,1,0:T(8,128)(2,1)S(1)} %all_to_all.20.weights_ref) | copy-start | bytes 28311556
  225.8 11.1 %copy-start.2 = (bf16[128,16,2048]{2,1,0:T(8,128)(2,1)}, bf16[128,16,2048]{2,1,0:T(8,128)(2,1)S(1)}, u32[]{:S(2)}) copy-start(bf16[128,16,2048]{2,1,0:T(8,128)(2,1)S(1)} %all_to_all.21.rows_ref) | copy-start | bytes 25165828
  236.9 5.5 %copy-start.4 = (s32[128,8]{0,1:T(8,128)S(1)}, s32[128,8]{0,1:T(8,128)}, u32[]{:S(2)}) copy-start(s32[128,8]{0,1:T(8,128)} %param.5) | copy-start | bytes 12292
  236.9 5.5 %copy-start.5 = (f32[128,8]{0,1:T(8,128)S(1)}, f32[128,8]{0,1:T(8,128)}, u32[]{:S(2)}) copy-start(f32[128,8]{0,1:T(8,128)} %param.6) | copy-start | bytes 12292
  236.9 58.5 %all-to-all-start.2 = ((bf16[128,8,2048]{2,1,0:T(8,128)(2,1)}), bf16[128,8,2048]{2,1,0:T(8,128)(2,1)}, u32[]{:S(2)}, u32[]{:S(2)}) async-start(bf16[128,8,2048]{2,1,0:T(8,128)(2,1)} %expert_ffn.3), calls=%async_computation.2 | async-start | bytes 8388608 | tf_op jit(solution)/shard_map/all_to_all | solution.py:202
  243.1 3.7 %copy-start.1 = (bf16[16,3,48,2048]{3,2,1,0:T(8,128)(2,1)S(1)}, bf16[16,3,48,2048]{3,2,1,0:T(8,128)(2,1)}, u32[]{:S(2)}) copy-start(bf16[16,3,48,2048]{3,2,1,0:T(8,128)(2,1)} %copy-done) | copy-start | bytes 28311556
  246.8 3.4 copy-start.3
  295.5 58.0 %all-to-all-start.3 = ((bf16[128,8,2048]{2,1,0:T(8,128)(2,1)}), bf16[128,8,2048]{2,1,0:T(8,128)(2,1)}, u32[]{:S(2)}, u32[]{:S(2)}) async-start(bf16[128,8,2048]{2,1,0:T(8,128)(2,1)} %expert_ffn.2), calls=%async_computation.3 | async-start | bytes 8388608 | tf_op jit(solution)/shard_map/all_to_all | solution.py:202

commit v7 on v5

--- a/solution.py
+++ b/solution.py
@@ -8,6 +8,7 @@
 from jax.sharding import PartitionSpec as P
 
 MOST = 16
+TILE = 256
 AXES = ("expert", "tensor")
 
 
@@ -56,7 +57,7 @@
     part = 64
     return pl.pallas_call(
         functools.partial(dispatch_kernel, first),
-        out_shape=pltpu.HBM((experts, count, width), jnp.bfloat16),
+        out_shape=jax.ShapeDtypeStruct((experts, count, width), jnp.bfloat16),
         grid=(experts // part,),
         in_specs=[pl.BlockSpec(memory_space=pltpu.HBM)] * 2,
         out_specs=pl.BlockSpec((part, count, width), lambda i: (i, 0, 0)),
@@ -83,29 +84,27 @@
     blocks, _, width_block, model = weights_ref.shape
     hidden_units = blocks * width_block
     contract_last = (((1,), (1,)), ((), ()))
-    x = rows_ref[...]
     w_gate = weights_ref[:, 0].reshape(hidden_units, model)
     w_up = weights_ref[:, 1].reshape(hidden_units, model)
     w_down = weights_ref[:, 2].reshape(hidden_units, model)
-    gate = lax.dot_general(x, w_gate, contract_last, preferred_element_type=jnp.float32)
-    up = lax.dot_general(x, w_up, contract_last, preferred_element_type=jnp.float32)
-    hidden = (gate / (1.0 + jnp.exp(-gate)) * up).astype(jnp.bfloat16)
-    out_ref[...] = jnp.dot(hidden, w_down, preferred_element_type=jnp.float32).astype(jnp.bfloat16)
+    for tile in range(rows_ref.shape[0] // TILE):
+        here = pl.ds(tile * TILE, TILE)
+        x = rows_ref[here, :]
+        gate = lax.dot_general(x, w_gate, contract_last, preferred_element_type=jnp.float32)
+        up = lax.dot_general(x, w_up, contract_last, preferred_element_type=jnp.float32)
+        hidden = (gate / (1.0 + jnp.exp(-gate)) * up).astype(jnp.bfloat16)
+        out = jnp.dot(hidden, w_down, preferred_element_type=jnp.float32)
+        out_ref[here, :] = out.astype(jnp.bfloat16)
 
 
 def expert_ffn(rows, weights):
     count, model = rows.shape
-    part = 256
     return pl.pallas_call(
         ffn_kernel,
         out_shape=jax.ShapeDtypeStruct((count, model), jnp.bfloat16),
-        grid=(count // part,),
-        in_specs=[
-            pl.BlockSpec((part, model), lambda i: (i, 0)),
-            pl.BlockSpec(weights.shape, lambda i: (0, 0, 0, 0), pipeline_mode=pl.Buffered(1)),
-        ],
-        out_specs=pl.BlockSpec((part, model), lambda i: (i, 0)),
-        compiler_params=pltpu.CompilerParams(vmem_limit_bytes=48 << 20),
+        in_specs=[pl.BlockSpec(memory_space=pltpu.VMEM)] * 2,
+        out_specs=pl.BlockSpec(memory_space=pltpu.VMEM),
+        compiler_params=pltpu.CompilerParams(vmem_limit_bytes=20 << 20),
         cost_estimate=pl.CostEstimate(
             flops=2 * count * weights.size,
             bytes_accessed=2 * (2 * rows.size + weights.size),
@@ -152,39 +151,33 @@
     )(ids_t, gates_t)
 
 
-def combine_kernel(weight_ref, values_ref, *refs):
-    *start_refs, out_ref = refs
-    rows = out_ref.shape[0]
-    sums = jnp.dot(weight_ref[...], values_ref[...], preferred_element_type=jnp.float32)
-    total = sums[:rows] + sums[rows:]
-    if start_refs:
-        total = start_refs[0][...] + total
-    out_ref[...] = total.astype(out_ref.dtype)
-
-
-def combine(weight, values, start, dtype):
+def combine_kernel(weight_ref, values_ref, out_ref):
+    rows, width = out_ref.shape
+    part = 512
+    for first in range(0, width, part):
+        here = pl.ds(first, part)
+        sums = jnp.dot(
+            weight_ref[...], values_ref[:, here], preferred_element_type=jnp.float32
+        )
+        out_ref[:, here] = (sums[:rows] + sums[rows:]).astype(out_ref.dtype)
+
+
+def combine(weight, values):
     depth, width = values.shape
     rows = weight.shape[0] // 2
-    part = 1024
-    column = pl.BlockSpec((rows, part), lambda i: (0, i))
     return pl.pallas_call(
         combine_kernel,
-        out_shape=jax.ShapeDtypeStruct((rows, width), dtype),
-        grid=(width // part,),
-        in_specs=[
-            pl.BlockSpec(weight.shape, lambda i: (0, 0)),
-            pl.BlockSpec((depth, part), lambda i: (0, i)),
-        ]
-        + [column] * len(start),
-        out_specs=column,
-        compiler_params=pltpu.CompilerParams(vmem_limit_bytes=32 << 20),
+        out_shape=jax.ShapeDtypeStruct((rows, width), jnp.bfloat16),
+        in_specs=[pl.BlockSpec(memory_space=pltpu.VMEM)] * 2,
+        out_specs=pl.BlockSpec(memory_space=pltpu.VMEM),
+        compiler_params=pltpu.CompilerParams(vmem_limit_bytes=16 << 20),
         cost_estimate=pl.CostEstimate(
             flops=2 * weight.size * width,
             bytes_accessed=2 * (depth + rows) * width,
             transcendentals=0,
         ),
         name="combine",
-    )(weight, values, *start)
+    )(weight, values)
 
 
 def exchange(rows):
@@ -197,25 +190,17 @@
     model = tokens.shape[1]
     ids_t = expert_ids.T
     gates_t = route_gates.T
-    half = MOST // 2
-    out_a = dispatch(ids_t, tokens, experts, 0, half)
-    out_b = dispatch(ids_t, tokens, experts, half, half)
-    in_a = exchange(out_a)
-    in_a, out_b, expert_weights = lax.optimization_barrier((in_a, out_b, expert_weights))
+    outgoing = dispatch(ids_t, tokens, experts, 0, MOST)
+    outgoing, expert_weights = lax.optimization_barrier((outgoing, expert_weights))
     weights = lax.all_to_all(expert_weights, "tensor", split_axis=0, concat_axis=0, tiled=True)
-    in_a, out_b, weights = lax.optimization_barrier((in_a, out_b, weights))
-    in_b = exchange(out_b)
-    done_a = expert_ffn(in_a.reshape(experts * half, model), weights)
-    done_a, in_b, ids_t, gates_t = lax.optimization_barrier((done_a, in_b, ids_t, gates_t))
-    back_a = exchange(done_a.reshape(experts, half, model))
-    done_b = expert_ffn(in_b.reshape(experts * half, model), weights)
-    gates_a, gates_b = coefficients(ids_t, gates_t, experts, 2)
-    done_b, back_a, gates_a, gates_b = lax.optimization_barrier(
-        (done_b, back_a, gates_a, gates_b)
-    )
-    back_b = exchange(done_b.reshape(experts, half, model))
-    part = combine(gates_a, back_a.reshape(experts * half, model), (), jnp.float32)
-    return combine(gates_b, back_b.reshape(experts * half, model), (part,), jnp.bfloat16)
+    outgoing, weights = lax.optimization_barrier((outgoing, weights))
+    arrived = exchange(outgoing)
+    arrived, ids_t, gates_t = lax.optimization_barrier((arrived, ids_t, gates_t))
+    (gates,) = coefficients(ids_t, gates_t, experts, 1)
+    outputs = expert_ffn(arrived.reshape(experts * MOST, model), weights)
+    outputs, gates = lax.optimization_barrier((outputs, gates))
+    returned = exchange(outputs.reshape(experts, MOST, model))
+    return combine(gates, returned.reshape(experts * MOST, model))
 
 
 def solution(mesh):

time: 361 us -> 355 us (0.983)
  blocking collectives: 111 us -> 327 us
  waiting for transfers between devices: 172 us -> 0 us
  starting transfers between devices: 28.8 us -> 0 us
  Pallas kernels: 44.3 us -> 27.3 us
  local copies, waits for them, and re-layouts: 3.94 us -> 0.01 us
    all_to_all x0 -> x2, blocking collectives: none -> 211 us  [exchange(): return lax.all_to_all(rows, AXES, split_axis=0, concat_axis=0, tiled=True)]
    all_to_all x4 -> x0, waiting for transfers between devices: 172 us -> none  [exchange(): return lax.all_to_all(rows, AXES, split_axis=0, concat_axis=0, tiled=True)]
    all_to_all x4 -> x0, starting transfers between devices: 28.8 us -> none  [exchange(): return lax.all_to_all(rows, AXES, split_axis=0, concat_axis=0, tiled=True)]
    pallas_call x2 -> x1, Pallas kernels: 29.3 us -> 19.9 us  [expert_ffn(): pl.pallas_call(ffn_kernel, out_shape=jax.ShapeDtypeStruct((count, model),...]
    all_to_all x1, blocking collectives: 111 us -> 116 us  [body(): lax.all_to_all(expert_weights, 'tensor', split_axis=0, concat_axis=0, til...]
    pallas_call x2 -> x1, Pallas kernels: 7.57 us -> 3.56 us  [dispatch(): pl.pallas_call(functools.partial(dispatch_kernel, first), out_shape=jax.S...]
    unnamed x8 -> x4, local copies, waits for them, and re-layouts: 3.94 us -> 0.01 us
    pallas_call x2 -> x1, Pallas kernels: 6.84 us -> 3.18 us  [combine(): pl.pallas_call(combine_kernel, out_shape=jax.ShapeDtypeStruct((rows, widt...]
  transfers between devices with their start and end apart: 4 -> 0, of which waited for: 4 -> 0; matrix products, arithmetic and copies ran while one was open for 0% -> 0% of each run, Pallas kernels for 10% -> 0%
where the time goes in v7:
time: 355 us; the launch traced here: 354 us
  blocking collectives  327 us (92%)
  Pallas kernels  27.3 us (8%)
    all_to_all x2, blocking collectives, exchange(): return lax.all_to_all(rows, AXES, split_axis=0, concat_axis=0, tiled=True)  211 us
    all_to_all x1, blocking collectives, body(): lax.all_to_all(expert_weights, 'tensor', split_axis=0, concat_axis=0, til...  116 us
    pallas_call x1, Pallas kernels, expert_ffn(): pl.pallas_call(ffn_kernel, out_shape=jax.ShapeDtypeStruct((count, model),...  19.9 us

profile of v7, /device:TPU:6, one launch (start us, length us, event | category | flops | bytes accessed | tf_op | source)
XLA Modules:
  0.0 354.4 jit_solution(7343201906479186300)
XLA Ops:
  0.0 3.6 %dispatch.1 = bf16[128,16,2048]{2,1,0:T(8,128)(2,1)S(1)} custom-call(s32[8,128]{1,0:T(8,128)} %bitcast.8, bf16[128,2048]{1,0:T(8,128)(2,1)} %tokens_hbm.1), custom_call_target="tpu_custom_call" | custom-call | flops 1073741824 | bytes 8912896 | tf_op jit(solution)/shard_map/dispatch/pallas_call | solution.py:58
  3.6 115.8 %all_to_all.15.weights_ref = bf16[16,3,48,2048]{3,2,1,0:T(8,128)(2,1)S(1)} all-to-all(bf16[16,3,48,2048]{3,2,1,0:T(8,128)(2,1)} %param.7), channel_id=1, replica_groups=mesh['expert'=8,'tensor'=16] {'tensor'}, dimensions={0} | all-to-all | bytes 18874368 | tf_op jit(solution)/shard_map/all_to_all | solution.py:195
  119.4 106.4 %all_to_all.16 = bf16[128,16,2048]{2,1,0:T(8,128)(2,1)S(1)} all-to-all(bf16[128,16,2048]{2,1,0:T(8,128)(2,1)S(1)} %dispatch.1), channel_id=1, replica_groups=mesh['expert'=8,'tensor'=16] {'expert','tensor'}, dimensions={0} | all-to-all | bytes 16777216 | tf_op jit(solution)/shard_map/all_to_all | solution.py:184
  225.8 0.0 copy-start
  225.8 0.0 copy-start.1
  225.8 19.9 %expert_ffn.1 = bf16[2048,2048]{1,0:T(8,128)(2,1)S(1)} custom-call(bf16[2048,2048]{1,0:T(8,128)(2,1)S(1)} %bitcast.7, bf16[16,3,48,2048]{3,2,1,0:T(8,128)(2,1)S(1)} %all_to_all.15.weights_ref), custom_call_target="tpu_custom_call" | custom-call | flops 19327352832 | bytes 26214400 | tf_op jit(solution)/shard_map/expert_ffn/pallas_call | solution.py:102
  245.8 0.0 copy-done
  245.8 0.0 copy-done.1
  245.8 0.6 coefficients.1.weight_ref
  246.4 104.9 %all_to_all.17 = bf16[128,16,2048]{2,1,0:T(8,128)(2,1)S(1)} all-to-all(bf16[128,16,2048]{2,1,0:T(8,128)(2,1)S(1)} %bitcast.6), channel_id=1, replica_groups=mesh['expert'=8,'tensor'=16] {'expert','tensor'}, dimensions={0} | all-to-all | bytes 16777216 | tf_op jit(solution)/shard_map/all_to_all | solution.py:184
  351.2 3.2 combine.1
Async XLA Ops:
  225.8 19.9 %copy-start = (s32[128,8]{0,1:T(8,128)S(1)}, s32[128,8]{0,1:T(8,128)}, u32[]{:S(2)}) copy-start(s32[128,8]{0,1:T(8,128)} %param.5) | copy-start | bytes 12292
  225.8 19.9 %copy-start.1 = (f32[128,8]{0,1:T(8,128)S(1)}, f32[128,8]{0,1:T(8,128)}, u32[]{:S(2)}) copy-start(f32[128,8]{0,1:T(8,128)} %param.6) | copy-start | bytes 12292

commit v8 on v7

--- a/solution.py
+++ b/solution.py
@@ -10,6 +10,11 @@
 MOST = 16
 TILE = 256
 AXES = ("expert", "tensor")
+
+
+def places(ids, grid):
+    groups, tensors = grid
+    return lax.rem(ids, tensors) * groups + lax.div(ids, tensors)
 
 
 def slot_codes(ids_t, experts):
@@ -29,7 +34,7 @@
     return jnp.where(member, rank, -1.0)
 
 
-def dispatch_kernel(first, ids_hbm, tokens_hbm, out_ref, ids_ref, tokens_ref, code_ref, sem):
+def dispatch_kernel(first, grid, ids_hbm, tokens_hbm, out_ref, ids_ref, tokens_ref, code_ref, sem):
     part, count, width = out_ref.shape
     step = pl.program_id(0)
 
@@ -40,7 +45,7 @@
         load_ids.start()
         load_tokens.start()
         load_ids.wait()
-        code_ref[...] = slot_codes(ids_ref[...], code_ref.shape[0])
+        code_ref[...] = slot_codes(places(ids_ref[...], grid), code_ref.shape[0])
         load_tokens.wait()
 
     code = code_ref[pl.ds(pl.multiple_of(step * part, part), part), :]
@@ -52,11 +57,11 @@
     out_ref[...] = picked.reshape(out_ref.shape).astype(jnp.bfloat16)
 
 
-def dispatch(ids_t, tokens, experts, first, count):
+def dispatch(ids_t, tokens, experts, first, count, grid):
     rows, width = tokens.shape
     part = 64
     return pl.pallas_call(
-        functools.partial(dispatch_kernel, first),
+        functools.partial(dispatch_kernel, first, grid),
         out_shape=jax.ShapeDtypeStruct((experts, count, width), jnp.bfloat16),
         grid=(experts // part,),
         in_specs=[pl.BlockSpec(memory_space=pltpu.HBM)] * 2,
@@ -114,9 +119,9 @@
     )(rows, weights)
 
 
-def coefficients_kernel(ids_ref, gates_ref, *out_refs):
+def coefficients_kernel(grid, ids_ref, gates_ref, *out_refs):
     experts = out_refs[0].shape[1] // (MOST // len(out_refs))
-    ids_t = ids_ref[...]
+    ids_t = places(ids_ref[...], grid)
     rows = ids_t.shape[1]
     code = slot_codes(ids_t, experts)
     names = lax.broadcasted_iota(jnp.int32, (experts, rows), 0)
@@ -135,11 +140,11 @@
         first += count
 
 
-def coefficients(ids_t, gates_t, experts, pieces):
+def coefficients(ids_t, gates_t, experts, pieces, grid):
     rows = ids_t.shape[1]
     width = experts * MOST // pieces
     return pl.pallas_call(
-        coefficients_kernel,
+        functools.partial(coefficients_kernel, grid),
         out_shape=[jax.ShapeDtypeStruct((2 * rows, width), jnp.bfloat16)] * pieces,
         compiler_params=pltpu.CompilerParams(vmem_limit_bytes=32 << 20),
         cost_estimate=pl.CostEstimate(
@@ -181,22 +186,23 @@
 
 
 def exchange(rows):
-    return lax.all_to_all(rows, AXES, split_axis=0, concat_axis=0, tiled=True)
+    return lax.all_to_all(rows, ("tensor", "expert"), split_axis=0, concat_axis=0, tiled=True)
 
 
 def body(tokens, expert_ids, route_gates, expert_weights):
     groups = lax.axis_size("expert")
     experts = expert_weights.shape[0] * groups
     model = tokens.shape[1]
+    grid = (groups, lax.axis_size("tensor"))
     ids_t = expert_ids.T
     gates_t = route_gates.T
-    outgoing = dispatch(ids_t, tokens, experts, 0, MOST)
+    outgoing = dispatch(ids_t, tokens, experts, 0, MOST, grid)
     outgoing, expert_weights = lax.optimization_barrier((outgoing, expert_weights))
     weights = lax.all_to_all(expert_weights, "tensor", split_axis=0, concat_axis=0, tiled=True)
     outgoing, weights = lax.optimization_barrier((outgoing, weights))
     arrived = exchange(outgoing)
     arrived, ids_t, gates_t = lax.optimization_barrier((arrived, ids_t, gates_t))
-    (gates,) = coefficients(ids_t, gates_t, experts, 1)
+    (gates,) = coefficients(ids_t, gates_t, experts, 1, grid)
     outputs = expert_ffn(arrived.reshape(experts * MOST, model), weights)
     outputs, gates = lax.optimization_barrier((outputs, gates))
     returned = exchange(outputs.reshape(experts, MOST, model))

time: 355 us -> 353 us (level)
  no operation moved by 1% of the time
where the time goes in v8:
time: 353 us; the launch traced here: 351 us
  blocking collectives  324 us (92%)
  Pallas kernels  27.3 us (8%)
    all_to_all x2, blocking collectives, exchange(): lax.all_to_all(rows, ('tensor', 'expert'), split_axis=0, concat_axis=0, t...  208 us
    all_to_all x1, blocking collectives, body(): lax.all_to_all(expert_weights, 'tensor', split_axis=0, concat_axis=0, til...  116 us
    pallas_call x1, Pallas kernels, expert_ffn(): pl.pallas_call(ffn_kernel, out_shape=jax.ShapeDtypeStruct((count, model),...  19.9 us

profile of v8, /device:TPU:6, one launch (start us, length us, event | category | flops | bytes accessed | tf_op | source)
XLA Modules:
  0.0 351.0 jit_solution(1077237436463301229)
XLA Ops:
  0.0 3.6 %dispatch.1 = bf16[128,16,2048]{2,1,0:T(8,128)(2,1)S(1)} custom-call(s32[8,128]{1,0:T(8,128)} %bitcast.8, bf16[128,2048]{1,0:T(8,128)(2,1)} %tokens_hbm.1), custom_call_target="tpu_custom_call" | custom-call | flops 1073741824 | bytes 8912896 | tf_op jit(solution)/shard_map/dispatch/pallas_call | solution.py:63
  3.6 115.8 %all_to_all.15.weights_ref = bf16[16,3,48,2048]{3,2,1,0:T(8,128)(2,1)S(1)} all-to-all(bf16[16,3,48,2048]{3,2,1,0:T(8,128)(2,1)} %param.7), channel_id=1, replica_groups=mesh['expert'=8,'tensor'=16] {'tensor'}, dimensions={0} | all-to-all | bytes 18874368 | tf_op jit(solution)/shard_map/all_to_all | solution.py:201
  119.4 103.4 %all_to_all.16 = bf16[128,16,2048]{2,1,0:T(8,128)(2,1)S(1)} all-to-all(bf16[128,16,2048]{2,1,0:T(8,128)(2,1)S(1)} %dispatch.1), channel_id=1, replica_groups=mesh['expert'=8,'tensor'=16] {'tensor','expert'}, dimensions={0} | all-to-all | bytes 16777216 | tf_op jit(solution)/shard_map/all_to_all | solution.py:189
  222.8 0.0 copy-start
  222.8 0.0 copy-start.1
  222.8 19.9 %expert_ffn.1 = bf16[2048,2048]{1,0:T(8,128)(2,1)S(1)} custom-call(bf16[2048,2048]{1,0:T(8,128)(2,1)S(1)} %bitcast.7, bf16[16,3,48,2048]{3,2,1,0:T(8,128)(2,1)S(1)} %all_to_all.15.weights_ref), custom_call_target="tpu_custom_call" | custom-call | flops 19327352832 | bytes 26214400 | tf_op jit(solution)/shard_map/expert_ffn/pallas_call | solution.py:107
  242.7 0.0 copy-done
  242.7 0.0 copy-done.1
  242.7 0.6 coefficients.1.weight_ref
  243.3 104.5 %all_to_all.17 = bf16[128,16,2048]{2,1,0:T(8,128)(2,1)S(1)} all-to-all(bf16[128,16,2048]{2,1,0:T(8,128)(2,1)S(1)} %bitcast.6), channel_id=1, replica_groups=mesh['expert'=8,'tensor'=16] {'tensor','expert'}, dimensions={0} | all-to-all | bytes 16777216 | tf_op jit(solution)/shard_map/all_to_all | solution.py:189
  347.9 3.2 combine.1
Async XLA Ops:
  222.8 19.9 %copy-start = (s32[128,8]{0,1:T(8,128)S(1)}, s32[128,8]{0,1:T(8,128)}, u32[]{:S(2)}) copy-start(s32[128,8]{0,1:T(8,128)} %param.5) | copy-start | bytes 12292
  222.8 19.9 %copy-start.1 = (f32[128,8]{0,1:T(8,128)S(1)}, f32[128,8]{0,1:T(8,128)}, u32[]{:S(2)}) copy-start(f32[128,8]{0,1:T(8,128)} %param.6) | copy-start | bytes 12292
